TPU v7x, 256 devices: a whole 4x4x8 slice. The times are simulated.
256 devices in a mesh: section: 4 (over z_hi, core), dp: 64 (over z_lo, y, x).
Axes of the slice: x: 4, y: 4, z: 8 (z_hi: 2, z_lo: 4; z = z_hi * 4 + z_lo), core: 2. Of those that a mesh axis runs over, the one named last changes fastest.
Arguments:
- layer_inputs: bfloat16 [4, 64, 512, 4096], P('section', 'dp'), may hold values from -6 to 6
- out_grads: bfloat16 [4, 64, 512, 4096], P('section', 'dp'), may hold values from -6 to 6
- projections: bfloat16 [4, 4096, 128], P('section'), may hold values from -0.09375 to 0.09375
- query_grads: bfloat16 [4, 2048, 4096], P('section', 'dp'), may hold values from -0.59765625 to 0.59765625
- lengths: int32 [64], P('dp'), may hold values from 1 to 512, as said below
Outputs:
- scores: float32 [64, 2048], P('dp', 'section')
Inputs may be any that keep to these rules, and one draw needn't show every extreme that they name: `lengths`: some training example fills all 512 slots.
All inputs are finite; a program needn't handle non-finite values.
Results may differ from a plain program's by a relative error of at most 0.005.
Values may be sent and summed in bfloat16 or wider, within the bound.
No kernel may reach another device: no remote copies, remote signals or barrier semaphores. Data moves between devices by JAX's collectives and lax.ppermute only.
A program may use at most 128 MiB of HBM per device.

v0:
```python
import jax
import jax.numpy as jnp
from jax import lax
from jax.sharding import PartitionSpec as P


def project_layer(inputs, grads, proj_table, valid_mask, token_count):
    low_rank = proj_table.shape[1] // 2
    ex_rows, seq_len, model_width = inputs.shape
    input_side = jnp.dot(
        inputs.reshape(ex_rows * seq_len, model_width),
        proj_table[:, :low_rank],
        preferred_element_type=jnp.float32,
    )
    input_side = input_side.astype(jnp.bfloat16).reshape(ex_rows, seq_len, low_rank)
    grad_side = jnp.dot(
        grads.reshape(ex_rows * seq_len, model_width),
        proj_table[:, low_rank:],
        preferred_element_type=jnp.float32,
    )
    grad_side = grad_side.astype(jnp.bfloat16).reshape(ex_rows, seq_len, low_rank)
    masked = grad_side * valid_mask[:, :, None]
    summed = (
        jnp.einsum("esa,esb->eab", masked, input_side, preferred_element_type=jnp.float32)
        / token_count[:, None, None]
    )
    return summed.astype(jnp.bfloat16).reshape(ex_rows, low_rank * low_rank)


def on_device(layer_inputs, out_grads, projections, query_grads, lengths):
    seq_len = layer_inputs.shape[2]
    valid_mask = (
        lax.broadcasted_iota(jnp.int32, (lengths.shape[0], seq_len), 1) < lengths[:, None]
    ).astype(jnp.bfloat16)
    token_count = lengths.astype(jnp.float32)
    example_grads = jnp.stack(
        [project_layer(layer_inputs[0], out_grads[0], projections[0], valid_mask, token_count)]
    )
    score_block = jnp.einsum(
        "ler,lqr->eq",
        lax.all_gather(example_grads, "dp", axis=1, tiled=True),
        query_grads,
        preferred_element_type=jnp.float32,
    )
    partial_value = lax.all_to_all(score_block, "dp", split_axis=0, concat_axis=1, tiled=True)
    return lax.psum_scatter(partial_value, "section", scatter_dimension=1, tiled=True)


def solution(mesh):
    placed = (
        P("section", "dp", None, None),
        P("section", "dp", None, None),
        P("section", None, None),
        P("section", "dp", None),
        P("dp"),
    )
    return jax.shard_map(
        on_device, mesh=mesh, in_specs=placed, out_specs=P("dp", "section"), check_vma=False
    )
```

profile of v0, /device:TPU:1, one launch (start us, length us, event | category | flops | bytes accessed | tf_op | source)
XLA Modules:
  0.0 278.2 jit_solution(2024502826622382864)
XLA Ops:
  6.5 0.0 copy-start
  6.5 0.0 copy-start.1
  6.5 0.0 reduce-scatter.4.cloned.1.call-start
  7.3 4.2 %fusion.13 = bf16[512,64]{0,1:T(8,128)(2,1)S(1)} fusion(bf16[1,1,512,4096]{3,2,1,0:T(8,128)(2,1)} %param.6, bf16[4096,128]{1,0:T(8,128)(2,1)} %bitcast.34, bf16[512]{0:T(512)(128)(2,1)S(1)} %fusion.29), kind=kOutput, calls=%fused_computation.7 | convolution fusion | flops 268500992 | bytes 5309440 | tf_op jit(solution)/shard_map/dot_general | solution.py:16
  11.5 0.0 copy-done.1
  11.5 3.7 %fusion.19 = bf16[64,64]{1,0:T(8,128)(2,1)S(1)} fusion(bf16[512,64]{0,1:T(8,128)(2,1)S(1)} %fusion.13, bf16[1,1,512,4096]{3,2,1,0:T(8,128)(2,1)} %param.5, bf16[4096,128]{1,0:T(8,128)(2,1)S(1)} %bitcast.35, f32[]{:T(128)} %bitcast.4), kind=kOutput, calls=%fused_computation.9 | convolution fusion | flops 272670720 | bytes 5316612 | tf_op jit(solution)/shard_map/esa,esb->eab/dot_general | solution.py:24
  15.3 0.1 stack_reshape.3
  15.3 166.6 %all_gather.3 = bf16[1,64,4096]{2,0,1:T(2,128)(2,1)S(1)} all-gather(bf16[1,1,4096]{2,0,1:T(2,128)(2,1)S(1)} %bitcast.38), channel_id=1, replica_groups=mesh['section'=4,'dp'=64] {'dp'}, dimensions={1}, use_global_device_ids=true | all-gather | bytes 532480 | tf_op jit(solution)/shard_map/all_gather | solution.py:41
  181.9 0.0 copy-done
  181.9 0.7 fusion.25
  182.6 12.8 %all_to_all.17 = f32[64,1,32]{2,1,0:T(1,128)S(1)} all-to-all(f32[64,1,32]{2,1,0:T(1,128)S(1)} %bitcast.39), channel_id=1, replica_groups=mesh['section'=4,'dp'=64] {'dp'}, dimensions={0} | all-to-all | bytes 16384 | tf_op jit(solution)/shard_map/all_to_all | solution.py:45
  195.4 0.5 broadcast.14
  195.9 0.7 reduce.3
  196.7 2.1 all_to_all.15
  198.7 0.0 reduce-scatter.4.cloned.1.call-update
  198.8 71.0 %reduce-scatter.4.cloned.1.call-done = f32[512,1]{1,0:T(8,128)} async-done(((f32[2048,1]{1,0:T(8,128)}), f32[512,1]{1,0:T(8,128)}) %reduce-scatter.4.cloned.1.call-update) | async-done | bytes 2064
  269.7 1.6 copy.12
  (1 shorter events, 0.0 us)
Async XLA Ops:
  6.5 175.4 %copy-start = (bf16[1,32,4096]{2,1,0:T(8,128)(2,1)S(1)}, bf16[1,32,4096]{2,1,0:T(8,128)(2,1)}, u32[]{:S(2)}) copy-start(bf16[1,32,4096]{2,1,0:T(8,128)(2,1)} %param.8) | copy-start | bytes 786436
  6.5 5.0 %copy-start.1 = (bf16[1,4096,128]{2,1,0:T(8,128)(2,1)S(1)}, bf16[1,4096,128]{2,1,0:T(8,128)(2,1)}, u32[]{:S(2)}) copy-start(bf16[1,4096,128]{2,1,0:T(8,128)(2,1)} %param.7) | copy-start | bytes 3145732
  6.5 263.2 %reduce-scatter.4.cloned.1.call-start = ((), (), s32[]{:S(2)}) async-start(), calls=%async_computation.2 | async-start | bytes 1310720
Sparse Core Ops, SparseCore 0:
  198.9 70.7 reduce-scatter.3
where the time goes:
time: 278 us
  blocking collectives  179 us (64%)
  waiting for transfers between devices  71 us (26%)
  between operations  14.2 us (5%)
  matrix products  8.61 us (3%)
  local copies, waits for them, and re-layouts  4.32 us (2%)
    all_gather x1, blocking collectives, on_device(): lax.all_gather(example_grads, 'dp', axis=1, tiled=True)  167 us
    unnamed x2, waiting for transfers between devices  71 us
    all_to_all x1, blocking collectives, on_device(): lax.all_to_all(score_block, 'dp', split_axis=0, concat_axis=1, tiled=True)  12.8 us
  transfers between devices with their start and end apart: 1, of which 1 were waited for; matrix products, arithmetic and copies ran while one was open for 0% of the time, Pallas kernels for 0%

commit v1 on v0

v1 whole, which is shorter than its diff:
```python
import jax
import jax.numpy as jnp
from jax import lax
from jax.sharding import PartitionSpec as P

SIDE = 4
BOTH = ("section", "dp")


def project_layer(inputs, grads, proj_table, valid_mask, token_count):
    low_rank = proj_table.shape[1] // 2
    input_side = jnp.dot(inputs, proj_table[:, :low_rank], preferred_element_type=jnp.float32)
    grad_side = jnp.dot(grads, proj_table[:, low_rank:], preferred_element_type=jnp.float32)
    masked = grad_side.astype(jnp.bfloat16) * valid_mask[:, None]
    summed = (
        jnp.einsum(
            "sa,sb->ab", masked, input_side.astype(jnp.bfloat16), preferred_element_type=jnp.float32
        )
        / token_count
    )
    return summed.astype(jnp.bfloat16).reshape(1, 1, low_rank * low_rank)


def on_device(n_sections, n_dp, layer_inputs, out_grads, projections, query_grads, lengths):
    seq_len = layer_inputs.shape[2]
    n_lines = n_dp // SIDE
    index = lax.axis_index("dp")
    x_pos, z_pos = index % SIDE, index // (SIDE * SIDE)
    my_section = lax.axis_index("section")

    own = query_grads[0]
    blocks = [own]
    for k in range(1, SIDE):
        pairs = []
        for s in range(n_sections):
            for line in range(n_lines):
                base = s * n_dp + line * SIDE
                pairs += [(base + x, base + (x - k) % SIDE) for x in range(SIDE)]
        blocks.append(lax.ppermute(own, BOTH, pairs))

    valid_mask = (lax.iota(jnp.int32, seq_len) < lengths[0]).astype(jnp.bfloat16)
    example = project_layer(
        layer_inputs[0, 0], out_grads[0, 0], projections[0], valid_mask, lengths[0].astype(jnp.float32)
    )

    plane = [[line * SIDE + x for line in range(n_lines)] for x in range(SIDE)]
    examples = lax.all_to_all(
        jnp.broadcast_to(example, (n_lines,) + example.shape[1:]),
        "dp",
        0,
        0,
        tiled=True,
        axis_index_groups=plane,
    )[:, 0]

    parts = [
        lax.dot_general(examples, b, (((1,), (1,)), ((), ())), preferred_element_type=jnp.float32)
        for b in blocks
    ]
    width = own.shape[0]
    twice = jnp.concatenate(parts + parts, axis=1)
    scores = lax.dynamic_slice(
        twice, (0, ((SIDE - x_pos) % SIDE) * width), (n_lines, SIDE * width)
    )

    keep = (jnp.arange(n_sections) == z_pos)[:, None, None]
    send = jnp.where(keep, scores[None], 0.0).reshape(n_sections * n_lines, 1, SIDE * width)
    over = [
        [s * n_dp + line * SIDE + x for s in range(n_sections) for line in range(n_lines)]
        for x in range(SIDE)
    ]
    got = lax.all_to_all(send, BOTH, 0, 0, tiled=True, axis_index_groups=over)
    got = got.reshape(n_sections, n_sections, SIDE, SIDE * width)
    return got.sum((0, 1)).reshape(1, SIDE * SIDE * width)


def solution(mesh):
    placed = (
        P("section", "dp", None, None),
        P("section", "dp", None, None),
        P("section", None, None),
        P("section", "dp", None),
        P("dp"),
    )

    def body(*args):
        return on_device(mesh.shape["section"], mesh.shape["dp"], *args)

    return jax.shard_map(
        body, mesh=mesh, in_specs=placed, out_specs=P("dp", "section"), check_vma=False
    )
```

time: 278 us -> 56.9 us (0.20)
  blocking collectives: 179 us -> 19.7 us
  waiting for transfers between devices: 71 us -> 9 us
  starting transfers between devices: 0.01 us -> 14.1 us
  between operations: 14.2 us -> 0.84 us
    all_gather x1 -> x0, blocking collectives: 167 us -> none  [on_device(): lax.all_gather(example_grads, 'dp', axis=1, tiled=True)]
    unnamed x2 -> x0, waiting for transfers between devices: 71 us -> none
    all_to_all x0 -> x1, starting transfers between devices: none -> 9.18 us  [on_device(): lax.all_to_all(jnp.broadcast_to(example, (n_lines,) + example.shape[1:]),...]
    all_to_all x1, blocking collectives: 12.8 us -> 19.7 us  [on_device(): got = lax.all_to_all(send, BOTH, 0, 0, tiled=True, axis_index_groups=over)]
    ppermute x0 -> x3, waiting for transfers between devices: none -> 6.24 us  [on_device(): blocks.append(lax.ppermute(own, BOTH, pairs))]
    ppermute x0 -> x3, starting transfers between devices: none -> 4.9 us  [on_device(): blocks.append(lax.ppermute(own, BOTH, pairs))]
    dot_general x3 -> x6, matrix products: 8.61 us -> 8.77 us  [the longest x1 4.22 us: project_layer(): jnp.dot(grads, proj_table[:, low_rank:], preferred_element_type=jnp.float32)]
  transfers between devices with their start and end apart: 1 -> 4, of which waited for: 1 -> 2; matrix products, arithmetic and copies ran while one was open for 0% -> 2% of each run, Pallas kernels for 0% -> 0%
where the time goes in v1:
time: 56.9 us; the launch traced here: 56.7 us
  blocking collectives  19.7 us (35%)
  starting transfers between devices  14.1 us (25%)
  waiting for transfers between devices  9 us (16%)
  matrix products  8.77 us (15%)
  local copies, waits for them, and re-layouts  2.15 us (4%)
  other arithmetic  2.12 us (4%)
  between operations  0.84 us (1%)
    all_to_all x1, blocking collectives, on_device(): got = lax.all_to_all(send, BOTH, 0, 0, tiled=True, axis_index_groups=over)  19.7 us
    all_to_all x1, starting transfers between devices, on_device(): lax.all_to_all(jnp.broadcast_to(example, (n_lines,) + example.shape[1:]),...  9.18 us
    ppermute x3, waiting for transfers between devices, on_device(): blocks.append(lax.ppermute(own, BOTH, pairs))  6.24 us
    ppermute x3, starting transfers between devices, on_device(): blocks.append(lax.ppermute(own, BOTH, pairs))  4.9 us
    dot_general x1, matrix products, project_layer(): jnp.dot(grads, proj_table[:, low_rank:], preferred_element_type=jnp.float32)  4.22 us
    dot_general x1, matrix products, project_layer(): jnp.einsum('sa,sb->ab', masked, input_side.astype(jnp.bfloat16), preferre...  3.76 us
    all_to_all x1, waiting for transfers between devices, on_device(): lax.all_to_all(jnp.broadcast_to(example, (n_lines,) + example.shape[1:]),...  2.76 us
    broadcast_in_dim x1, other arithmetic, on_device(): jnp.broadcast_to(example, (n_lines,) + example.shape[1:])  1.37 us
  transfers between devices with their start and end apart: 4, of which 2 were waited for; matrix products, arithmetic and copies ran while one was open for 2% of the time, Pallas kernels for 0%

profile of v1, /device:TPU:1, one launch (start us, length us, event | category | flops | bytes accessed | tf_op | source)
XLA Modules:
  0.0 56.7 jit_solution(1046978978813466694)
XLA Ops:
  0.0 0.0 copy-start
  0.8 4.2 %fusion.13 = bf16[512,64]{0,1:T(8,128)(2,1)S(1)} fusion(bf16[1,1,512,4096]{3,2,1,0:T(8,128)(2,1)} %param.6, bf16[4096,128]{1,0:T(8,128)(2,1)} %bitcast.41, bf16[512]{0:T(512)(128)(2,1)S(1)} %fusion.33), kind=kOutput, calls=%fused_computation.7 | convolution fusion | flops 268500992 | bytes 5309440 | tf_op jit(solution)/shard_map/dot_general | solution.py:13
  5.0 0.0 copy-done
  5.0 0.0 copy-start.1
  5.0 3.8 %fusion.19 = bf16[64,64]{1,0:T(8,128)(2,1)S(1)} fusion(bf16[512,64]{0,1:T(8,128)(2,1)S(1)} %fusion.13, bf16[1,1,512,4096]{3,2,1,0:T(8,128)(2,1)} %param.5, bf16[4096,128]{1,0:T(8,128)(2,1)S(1)} %bitcast.42, f32[]{:T(128)S(6)} %convert_element_type.22), kind=kOutput, calls=%fused_computation.9 | convolution fusion | flops 272670720 | bytes 5316612 | tf_op jit(solution)/shard_map/sa,sb->ab/dot_general | solution.py:16
  8.8 0.1 broadcast_in_dim.39
  8.8 0.2 broadcast_in_dim.40
  9.1 0.5 broadcast.36
  9.6 1.4 %reduce = bf16[16,4096]{1,0:T(8,128)(2,1)S(1)} reduce(bf16[16,1,4096]{2,1,0:T(2,128)(2,1)S(1)} %broadcast_in_dim.40, bf16[]{:T(256)} %broadcast.36), dimensions={1}, to_apply=%broadcast_in_dim.40.reduce_sub_computation | reduce | bytes 262146 | tf_op jit(solution)/shard_map/broadcast_in_dim | solution.py:48
  11.0 0.7 %reshape.57 = bf16[16,2,2048]{2,1,0:T(2,128)(2,1)} reshape(bf16[16,4096]{1,0:T(8,128)(2,1)S(1)} %reduce) | data formatting | bytes 262144
  11.7 9.2 %all-to-all-start = ((bf16[16,2,2048]{2,1,0:T(2,128)(2,1)}), bf16[16,2,2048]{2,1,0:T(2,128)(2,1)S(1)}, u32[]{:S(2)}, u32[]{:S(2)}) async-start(bf16[16,2,2048]{2,1,0:T(2,128)(2,1)} %reshape.57), calls=%async_computation | async-start | bytes 262144 | tf_op jit(solution)/shard_map/all_to_all | solution.py:47
  20.9 0.0 copy-done.1
  20.9 1.3 %collective-permute-start.2 = (bf16[32,4096]{1,0:T(8,128)(2,1)S(1)}, bf16[32,4096]{1,0:T(8,128)(2,1)S(1)}, u32[]{:S(2)}, u32[]{:S(2)}) collective-permute-start(bf16[32,4096]{1,0:T(8,128)(2,1)S(1)} %bitcast.43), channel_id=1, source_target_pairs={{0,1},{1,2},{2,3},{3,0},{4,5},{5,6},{6,7},{7,4},{8,9},{9,10},{10,1... | collective-permute-start | bytes 786440 | tf_op jit(solution)/shard_map/ppermute | solution.py:39
  22.2 2.5 %collective-permute-start.1 = (bf16[32,4096]{1,0:T(8,128)(2,1)S(1)}, bf16[32,4096]{1,0:T(8,128)(2,1)S(1)}, u32[]{:S(2)}, u32[]{:S(2)}) collective-permute-start(bf16[32,4096]{1,0:T(8,128)(2,1)S(1)} %bitcast.44), channel_id=1, source_target_pairs={{0,2},{1,3},{2,0},{3,1},{4,6},{5,7},{6,4},{7,5},{8,10},{9,11},{10,... | collective-permute-start | bytes 786440 | tf_op jit(solution)/shard_map/ppermute | solution.py:39
  24.6 1.2 %collective-permute-start = (bf16[32,4096]{1,0:T(8,128)(2,1)S(1)}, bf16[32,4096]{1,0:T(8,128)(2,1)S(1)}, u32[]{:S(2)}, u32[]{:S(2)}) collective-permute-start(bf16[32,4096]{1,0:T(8,128)(2,1)S(1)} %bitcast.45), channel_id=1, source_target_pairs={{0,3},{1,0},{2,1},{3,2},{4,7},{5,4},{6,5},{7,6},{8,11},{9,8},{10,9... | collective-permute-start | bytes 786440 | tf_op jit(solution)/shard_map/ppermute | solution.py:39
  25.8 0.1 broadcast_in_dim.36
  25.8 0.1 broadcast_in_dim.37
  25.9 2.8 %all-to-all-done = bf16[16,2,2048]{2,1,0:T(2,128)(2,1)S(1)} async-done(((bf16[16,2,2048]{2,1,0:T(2,128)(2,1)}), bf16[16,2,2048]{2,1,0:T(2,128)(2,1)S(1)}, u32[]{:S(2)}, u32[]{:S(2)}) %all-to-all-start) | async-done | bytes 131104 | tf_op jit(solution)/shard_map/all_to_all | solution.py:47
  28.7 0.1 reshape.58
  28.8 0.2 copy.6
  29.0 0.2 fusion.31
  29.2 0.0 collective-permute-done.2
  29.2 0.2 fusion.25
  29.4 6.2 %collective-permute-done.1 = bf16[32,4096]{1,0:T(8,128)(2,1)S(1)} collective-permute-done((bf16[32,4096]{1,0:T(8,128)(2,1)S(1)}, bf16[32,4096]{1,0:T(8,128)(2,1)S(1)}, u32[]{:S(2)}, u32[]{:S(2)}) %collective-permute-start.1) | collective-permute-done | bytes 262176 | tf_op jit(solution)/shard_map/ppermute | solution.py:39
  35.6 0.2 fusion.27
  35.8 0.0 collective-permute-done
  35.8 0.2 fusion.29
  36.0 0.1 concatenate.3
  36.1 0.1 constant_dynamic-slice_fusion
  36.2 0.1 broadcast_select_fusion
  36.4 19.7 %all_to_all.10 = f32[64,1,128]{2,1,0:T(1,128)S(1)} all-to-all(f32[64,1,128]{2,1,0:T(1,128)S(1)} %broadcast_select_fusion), channel_id=1, replica_groups={{0,4,8,12,16,20,24,28,32,36,40,44,48,52,56,60,64,68,72,76,80,84,88,92,9..., dimensions={0} | all-to-all | bytes 65536 | tf_op jit(solution)/shard_map/all_to_all | solution.py:72
  56.1 0.6 %reduce_sum.9 = f32[4,128]{1,0:T(4,128)} reduce(f32[4,4,4,128]{3,2,1,0:T(4,128)S(1)} %bitcast.47, f32[]{:T(128)} %constant.41.clone.1), dimensions={0,1}, to_apply=%region_0.1 | reduce | flops 7680 | bytes 34820 | tf_op jit(solution)/shard_map/reduce_sum | solution.py:74
  (3 shorter events, 0.0 us)
Async XLA Ops:
  0.0 5.0 %copy-start = (bf16[1,4096,128]{2,1,0:T(8,128)(2,1)S(1)}, bf16[1,4096,128]{2,1,0:T(8,128)(2,1)}, u32[]{:S(2)}) copy-start(bf16[1,4096,128]{2,1,0:T(8,128)(2,1)} %param.7) | copy-start | bytes 3145732
  5.0 15.9 %copy-start.1 = (bf16[1,32,4096]{2,1,0:T(8,128)(2,1)S(1)}, bf16[1,32,4096]{2,1,0:T(8,128)(2,1)}, u32[]{:S(2)}) copy-start(bf16[1,32,4096]{2,1,0:T(8,128)(2,1)} %param.8) | copy-start | bytes 786436
  11.7 17.0 %all-to-all-start = ((bf16[16,2,2048]{2,1,0:T(2,128)(2,1)}), bf16[16,2,2048]{2,1,0:T(2,128)(2,1)S(1)}, u32[]{:S(2)}, u32[]{:S(2)}) async-start(bf16[16,2,2048]{2,1,0:T(2,128)(2,1)} %reshape.57), calls=%async_computation | async-start | bytes 262144 | tf_op jit(solution)/shard_map/all_to_all | solution.py:47
  20.9 8.3 %collective-permute-start.2 = (bf16[32,4096]{1,0:T(8,128)(2,1)S(1)}, bf16[32,4096]{1,0:T(8,128)(2,1)S(1)}, u32[]{:S(2)}, u32[]{:S(2)}) collective-permute-start(bf16[32,4096]{1,0:T(8,128)(2,1)S(1)} %bitcast.43), channel_id=1, source_target_pairs={{0,1},{1,2},{2,3},{3,0},{4,5},{5,6},{6,7},{7,4},{8,9},{9,10},{10,1... | collective-permute-start | bytes 786440 | tf_op jit(solution)/shard_map/ppermute | solution.py:39
  22.2 13.5 %collective-permute-start.1 = (bf16[32,4096]{1,0:T(8,128)(2,1)S(1)}, bf16[32,4096]{1,0:T(8,128)(2,1)S(1)}, u32[]{:S(2)}, u32[]{:S(2)}) collective-permute-start(bf16[32,4096]{1,0:T(8,128)(2,1)S(1)} %bitcast.44), channel_id=1, source_target_pairs={{0,2},{1,3},{2,0},{3,1},{4,6},{5,7},{6,4},{7,5},{8,10},{9,11},{10,... | collective-permute-start | bytes 786440 | tf_op jit(solution)/shard_map/ppermute | solution.py:39
  24.6 11.2 %collective-permute-start = (bf16[32,4096]{1,0:T(8,128)(2,1)S(1)}, bf16[32,4096]{1,0:T(8,128)(2,1)S(1)}, u32[]{:S(2)}, u32[]{:S(2)}) collective-permute-start(bf16[32,4096]{1,0:T(8,128)(2,1)S(1)} %bitcast.45), channel_id=1, source_target_pairs={{0,3},{1,0},{2,1},{3,2},{4,7},{5,4},{6,5},{7,6},{8,11},{9,8},{10,9... | collective-permute-start | bytes 786440 | tf_op jit(solution)/shard_map/ppermute | solution.py:39

commit v2 on v1

v2 whole, which is shorter than its diff:
```python
import functools

import jax
import jax.numpy as jnp
from jax import lax
from jax.experimental import pallas as pl
from jax.experimental.pallas import tpu as pltpu
from jax.sharding import PartitionSpec as P

SIDE = 4
BOTH = ("section", "dp")
LANES = 128
CHUNKS = 4


def example_kernel(
    len_ref, in_hbm, grad_hbm, proj_hbm, out_ref, in_buf, grad_buf, proj_buf, staged, in_sem, grad_sem, proj_sem
):
    width = proj_buf.shape[0] // CHUNKS
    rank = proj_buf.shape[1] // 2
    copies = []
    for c in range(CHUNKS):
        cols = pl.ds(c * width, width)
        trio = (
            pltpu.make_async_copy(proj_hbm.at[0, cols, :], proj_buf.at[cols, :], proj_sem.at[c]),
            pltpu.make_async_copy(in_hbm.at[0, 0, :, cols], in_buf.at[:, cols], in_sem.at[c]),
            pltpu.make_async_copy(grad_hbm.at[0, 0, :, cols], grad_buf.at[:, cols], grad_sem.at[c]),
        )
        for copy in trio:
            copy.start()
        copies.append(trio)
    input_side = grad_side = None
    for c in range(CHUNKS):
        cols = slice(c * width, (c + 1) * width)
        for copy in copies[c]:
            copy.wait()
        table = proj_buf[cols, :]
        a = jnp.dot(in_buf[:, cols], table, preferred_element_type=jnp.float32)
        b = jnp.dot(grad_buf[:, cols], table, preferred_element_type=jnp.float32)
        input_side = a if input_side is None else input_side + a
        grad_side = b if grad_side is None else grad_side + b
    input_side = input_side[:, :rank].astype(jnp.bfloat16)
    grad_side = grad_side[:, rank:].astype(jnp.bfloat16)
    count = len_ref[0]
    real = lax.broadcasted_iota(jnp.int32, grad_side.shape, 0) < count
    grad_side = jnp.where(real, grad_side, jnp.zeros_like(grad_side))
    summed = lax.dot_general(
        grad_side, input_side, (((0,), (0,)), ((), ())), preferred_element_type=jnp.float32
    )
    staged[...] = summed / count.astype(jnp.float32)
    half = rank // 2
    flat = jnp.concatenate(
        [staged[pl.ds(0, half, stride=2), :], staged[pl.ds(1, half, stride=2), :]], axis=1
    ).astype(jnp.bfloat16)
    for i in range(out_ref.shape[0]):
        out_ref[i] = flat


def example_copies(n_copies, lengths, layer_inputs, out_grads, projections):
    tokens, model = layer_inputs.shape[2:]
    both = projections.shape[2]
    rank = both // 2
    hbm = pl.BlockSpec(memory_space=pltpu.HBM)
    return pl.pallas_call(
        example_kernel,
        out_shape=jax.ShapeDtypeStruct((n_copies, rank * rank // LANES, LANES), jnp.bfloat16),
        in_specs=[pl.BlockSpec(memory_space=pltpu.SMEM), hbm, hbm, hbm],
        out_specs=pl.BlockSpec(memory_space=pltpu.VMEM),
        scratch_shapes=[
            pltpu.VMEM((tokens, model), jnp.bfloat16),
            pltpu.VMEM((tokens, model), jnp.bfloat16),
            pltpu.VMEM((model, both), jnp.bfloat16),
            pltpu.VMEM((rank, rank), jnp.float32),
            pltpu.SemaphoreType.DMA((CHUNKS,)),
            pltpu.SemaphoreType.DMA((CHUNKS,)),
            pltpu.SemaphoreType.DMA((CHUNKS,)),
        ],
        compiler_params=pltpu.CompilerParams(vmem_limit_bytes=56 << 20),
        cost_estimate=pl.CostEstimate(
            flops=COST_FLOPS, bytes_accessed=9 << 20, transcendentals=0
        ),
        name="example_gradient",
    )(lengths, layer_inputs, out_grads, projections)


COST_FLOPS = 1 << 31


def score_kernel(n_sections, got_ref, *rest):
    block_refs, (out_ref, wide) = rest[:SIDE], rest[SIDE:]
    index = lax.axis_index("dp")
    x_pos, z_pos = lax.rem(index, SIDE), lax.div(index, SIDE * SIDE)
    n, rows, lanes = got_ref.shape
    wide[...] = got_ref[...].reshape(n * rows, lanes).astype(jnp.float32)
    examples = jnp.concatenate(
        [wide[pl.ds(c, n, stride=rows), :] for c in range(rows)], axis=1
    ).astype(jnp.bfloat16)
    queries = jnp.concatenate([b[...] for b in block_refs], axis=0)
    scores = lax.dot_general(
        examples, queries, (((1,), (1,)), ((), ())), preferred_element_type=jnp.float32
    )
    scores = pltpu.roll(scores, x_pos * (scores.shape[1] // SIDE), 1)
    for s in range(n_sections):
        out_ref[s * n : (s + 1) * n, :] = jnp.where(z_pos == s, scores, jnp.zeros_like(scores))


def score_rows(n_sections, examples, blocks):
    n, rows, lanes = examples.shape
    vmem = pl.BlockSpec(memory_space=pltpu.VMEM)
    return pl.pallas_call(
        functools.partial(score_kernel, n_sections),
        out_shape=jax.ShapeDtypeStruct((n_sections * n, SIDE * blocks[0].shape[0]), jnp.float32),
        in_specs=[vmem] * (1 + SIDE),
        out_specs=vmem,
        scratch_shapes=[pltpu.VMEM((n * rows, lanes), jnp.float32)],
        compiler_params=pltpu.CompilerParams(vmem_limit_bytes=8 << 20),
        name="scores",
    )(examples, *blocks)


def on_device(n_sections, n_dp, layer_inputs, out_grads, projections, query_grads, lengths):
    n_lines = n_dp // SIDE

    own = query_grads[0]
    blocks = [own]
    for k in range(1, SIDE):
        pairs = []
        for s in range(n_sections):
            for line in range(n_lines):
                base = s * n_dp + line * SIDE
                pairs += [(base + x, base + (x - k) % SIDE) for x in range(SIDE)]
        blocks.append(lax.ppermute(own, BOTH, pairs))

    plane = [[line * SIDE + x for line in range(n_lines)] for x in range(SIDE)]
    copies = example_copies(n_lines, lengths, layer_inputs, out_grads, projections)
    examples = lax.all_to_all(copies, "dp", 0, 0, tiled=True, axis_index_groups=plane)

    send = score_rows(n_sections, examples, blocks)
    over = [
        [s * n_dp + line * SIDE + x for s in range(n_sections) for line in range(n_lines)]
        for x in range(SIDE)
    ]
    got = lax.all_to_all(send[:, None], BOTH, 0, 0, tiled=True, axis_index_groups=over)
    got = got.reshape(n_sections, n_sections, SIDE, send.shape[1])
    return got.sum((0, 1)).reshape(1, SIDE * send.shape[1])


def solution(mesh):
    placed = (
        P("section", "dp", None, None),
        P("section", "dp", None, None),
        P("section", None, None),
        P("section", "dp", None),
        P("dp"),
    )

    def body(*args):
        return on_device(mesh.shape["section"], mesh.shape["dp"], *args)

    return jax.shard_map(
        body, mesh=mesh, in_specs=placed, out_specs=P("dp", "section"), check_vma=False
    )
```

time: 56.9 us -> 48.1 us (0.85)
  blocking collectives: 19.7 us -> 34.6 us
  waiting for transfers between devices: 9 us -> 0.01 us
  matrix products: 8.77 us -> 0 us
  starting transfers between devices: 14.1 us -> 5.64 us
  Pallas kernels: 0 us -> 6.35 us
  local copies, waits for them, and re-layouts: 2.15 us -> 0.01 us
  other arithmetic: 2.12 us -> 0.6 us
    all_to_all x1 -> x2, blocking collectives: 19.7 us -> 34.6 us  [the longest x1 18.4 us: on_device(): lax.all_to_all(send[:, None], BOTH, 0, 0, tiled=True, axis_index_groups=o...]
    all_to_all x1 -> x0, starting transfers between devices: 9.18 us -> none  [on_device(): lax.all_to_all(jnp.broadcast_to(example, (n_lines,) + example.shape[1:]),...]
    dot_general x6 -> x0, matrix products: 8.77 us -> none  [the longest x1 4.22 us: project_layer(): jnp.dot(grads, proj_table[:, low_rank:], preferred_element_type=jnp.float32)]
    pallas_call x0 -> x2, Pallas kernels: none -> 6.35 us  [the longest x1 5.9 us: example_copies(): pl.pallas_call(example_kernel, out_shape=jax.ShapeDtypeStruct((n_copies,...]
    ppermute x3, waiting for transfers between devices: 6.24 us -> 0.01 us  [on_device(): blocks.append(lax.ppermute(own, BOTH, pairs))]
    all_to_all x1 -> x0, waiting for transfers between devices: 2.76 us -> none  [on_device(): lax.all_to_all(jnp.broadcast_to(example, (n_lines,) + example.shape[1:]),...]
    broadcast_in_dim x1 -> x0, other arithmetic: 1.37 us -> none  [on_device(): jnp.broadcast_to(example, (n_lines,) + example.shape[1:])]
    unnamed x7 -> x2, local copies, waits for them, and re-layouts: 0.99 us -> 0.01 us
  transfers between devices with their start and end apart: 4 -> 3, of which waited for: 2 -> 0; matrix products, arithmetic and copies ran while one was open for 2% -> 0% of each run, Pallas kernels for 0% -> 12%
where the time goes in v2:
time: 48.1 us; the launch traced here: 47.9 us
  blocking collectives  34.6 us (72%)
  Pallas kernels  6.35 us (13%)
  starting transfers between devices  5.64 us (12%)
  between operations  0.68 us (1%)
  other arithmetic  0.6 us (1%)
    all_to_all x1, blocking collectives, on_device(): lax.all_to_all(send[:, None], BOTH, 0, 0, tiled=True, axis_index_groups=o...  18.4 us
    all_to_all x1, blocking collectives, on_device(): lax.all_to_all(copies, 'dp', 0, 0, tiled=True, axis_index_groups=plane)  16.1 us
    pallas_call x1, Pallas kernels, example_copies(): pl.pallas_call(example_kernel, out_shape=jax.ShapeDtypeStruct((n_copies,...  5.9 us
    ppermute x3, starting transfers between devices, on_device(): blocks.append(lax.ppermute(own, BOTH, pairs))  5.64 us
  transfers between devices with their start and end apart: 3, of which 0 were waited for; matrix products, arithmetic and copies ran while one was open for 0% of the time, Pallas kernels for 12%

profile of v2, /device:TPU:1, one launch (start us, length us, event | category | flops | bytes accessed | tf_op | source)
XLA Modules:
  0.0 47.9 jit_solution(18092440345499920503)
XLA Ops:
  0.0 2.0 %collective-permute-start.2 = (bf16[32,4096]{1,0:T(8,128)(2,1)}, bf16[32,4096]{1,0:T(8,128)(2,1)S(1)}, u32[]{:S(2)}, u32[]{:S(2)}) collective-permute-start(bf16[32,4096]{1,0:T(8,128)(2,1)} %bitcast.6), channel_id=1, source_target_pairs={{0,1},{1,2},{2,3},{3,0},{4,5},{5,6},{6,7},{7,4},{8,9},{9,10},{10,1... | collective-permute-start | bytes 786440 | tf_op jit(solution)/shard_map/ppermute | solution.py:132
  2.0 2.5 %collective-permute-start.1 = (bf16[32,4096]{1,0:T(8,128)(2,1)}, bf16[32,4096]{1,0:T(8,128)(2,1)S(1)}, u32[]{:S(2)}, u32[]{:S(2)}) collective-permute-start(bf16[32,4096]{1,0:T(8,128)(2,1)} %bitcast.7), channel_id=1, source_target_pairs={{0,2},{1,3},{2,0},{3,1},{4,6},{5,7},{6,4},{7,5},{8,10},{9,11},{10,... | collective-permute-start | bytes 786440 | tf_op jit(solution)/shard_map/ppermute | solution.py:132
  4.5 1.2 %collective-permute-start = (bf16[32,4096]{1,0:T(8,128)(2,1)}, bf16[32,4096]{1,0:T(8,128)(2,1)S(1)}, u32[]{:S(2)}, u32[]{:S(2)}) collective-permute-start(bf16[32,4096]{1,0:T(8,128)(2,1)} %bitcast.8), channel_id=1, source_target_pairs={{0,3},{1,0},{2,1},{3,2},{4,7},{5,4},{6,5},{7,6},{8,11},{9,8},{10,9... | collective-permute-start | bytes 786440 | tf_op jit(solution)/shard_map/ppermute | solution.py:132
  6.3 0.0 copy-start
  6.3 5.9 %example_gradient.1 = bf16[16,32,128]{2,1,0:T(8,128)(2,1)} custom-call(s32[1]{0:T(128)S(6)} %copy.7.len_ref, bf16[1,1,512,4096]{3,2,1,0:T(8,128)(2,1)} %in_hbm.1, bf16[1,1,512,4096]{3,2,1,0:T(8,128)(2,1)} %grad_hbm.1, bf16[1,4096,128]{2,1,0:T(8,128)(2,1)} %proj_hbm.1), custom_call_target="tpu_custom_call" | custom-call | flops 2147483648 | bytes 9437184 | tf_op jit(solution)/shard_map/example_gradient/pallas_call | solution.py:64
  12.2 16.1 %all_to_all.10.got_ref = bf16[16,32,128]{2,1,0:T(8,128)(2,1)S(1)} all-to-all(bf16[16,32,128]{2,1,0:T(8,128)(2,1)} %example_gradient.1), channel_id=1, replica_groups={{0,4,8,12,16,20,24,28,32,36,40,44,48,52,56,60},{1,5,9,13,17,21,25,29,33..., dimensions={0} | all-to-all | bytes 262144 | tf_op jit(solution)/shard_map/all_to_all | solution.py:136
  28.4 0.0 collective-permute-done.2.rest_3_
  28.4 0.0 collective-permute-done.1.rest_2_
  28.4 0.0 collective-permute-done.rest_1_
  28.4 0.0 copy-done
  28.4 0.5 scores.1
  28.8 18.4 %all_to_all.11 = f32[64,1,128]{2,1,0:T(1,128)S(1)} all-to-all(f32[64,1,128]{2,1,0:T(1,128)S(1)} %bitcast.10), channel_id=1, replica_groups={{0,4,8,12,16,20,24,28,32,36,40,44,48,52,56,60,64,68,72,76,80,84,88,92,9..., dimensions={0} | all-to-all | bytes 65536 | tf_op jit(solution)/shard_map/all_to_all | solution.py:143
  47.3 0.6 %reduce_sum.9 = f32[4,128]{1,0:T(4,128)} reduce(f32[4,4,4,128]{3,2,1,0:T(4,128)S(1)} %bitcast.11, f32[]{:T(128)} %constant.0.clone.1), dimensions={0,1}, to_apply=%region_0.0 | reduce | flops 7680 | bytes 34820 | tf_op jit(solution)/shard_map/reduce_sum | solution.py:145
Async XLA Ops:
  0.0 28.4 %collective-permute-start.2 = (bf16[32,4096]{1,0:T(8,128)(2,1)}, bf16[32,4096]{1,0:T(8,128)(2,1)S(1)}, u32[]{:S(2)}, u32[]{:S(2)}) collective-permute-start(bf16[32,4096]{1,0:T(8,128)(2,1)} %bitcast.6), channel_id=1, source_target_pairs={{0,1},{1,2},{2,3},{3,0},{4,5},{5,6},{6,7},{7,4},{8,9},{9,10},{10,1... | collective-permute-start | bytes 786440 | tf_op jit(solution)/shard_map/ppermute | solution.py:132
  2.0 26.3 %collective-permute-start.1 = (bf16[32,4096]{1,0:T(8,128)(2,1)}, bf16[32,4096]{1,0:T(8,128)(2,1)S(1)}, u32[]{:S(2)}, u32[]{:S(2)}) collective-permute-start(bf16[32,4096]{1,0:T(8,128)(2,1)} %bitcast.7), channel_id=1, source_target_pairs={{0,2},{1,3},{2,0},{3,1},{4,6},{5,7},{6,4},{7,5},{8,10},{9,11},{10,... | collective-permute-start | bytes 786440 | tf_op jit(solution)/shard_map/ppermute | solution.py:132
  4.5 23.9 %collective-permute-start = (bf16[32,4096]{1,0:T(8,128)(2,1)}, bf16[32,4096]{1,0:T(8,128)(2,1)S(1)}, u32[]{:S(2)}, u32[]{:S(2)}) collective-permute-start(bf16[32,4096]{1,0:T(8,128)(2,1)} %bitcast.8), channel_id=1, source_target_pairs={{0,3},{1,0},{2,1},{3,2},{4,7},{5,4},{6,5},{7,6},{8,11},{9,8},{10,9... | collective-permute-start | bytes 786440 | tf_op jit(solution)/shard_map/ppermute | solution.py:132
  6.3 22.1 %copy-start = (bf16[1,32,4096]{2,1,0:T(8,128)(2,1)S(1)}, bf16[1,32,4096]{2,1,0:T(8,128)(2,1)}, u32[]{:S(2)}) copy-start(bf16[1,32,4096]{2,1,0:T(8,128)(2,1)} %param.8) | copy-start | bytes 786436

commit v3 on v2

v3 whole, which is shorter than its diff:
```python
import functools

import jax
import jax.numpy as jnp
from jax import lax
from jax.experimental import pallas as pl
from jax.experimental.pallas import tpu as pltpu
from jax.sharding import PartitionSpec as P

SIDE = 4
BOTH = ("section", "dp")
LANES = 128


def example_kernel(len_ref, in_ref, grad_ref, proj_ref, out_ref, staged):
    rank = proj_ref.shape[2] // 2
    table = proj_ref[0]
    input_side = jnp.dot(in_ref[0, 0], table, preferred_element_type=jnp.float32)
    grad_side = jnp.dot(grad_ref[0, 0], table, preferred_element_type=jnp.float32)
    input_side = input_side[:, :rank].astype(jnp.bfloat16)
    grad_side = grad_side[:, rank:].astype(jnp.bfloat16)
    count = len_ref[0]
    real = lax.broadcasted_iota(jnp.int32, grad_side.shape, 0) < count
    grad_side = jnp.where(real, grad_side, jnp.zeros_like(grad_side))
    summed = lax.dot_general(
        grad_side, input_side, (((0,), (0,)), ((), ())), preferred_element_type=jnp.float32
    )
    staged[...] = summed / count.astype(jnp.float32)
    half = rank // 2
    flat = jnp.concatenate(
        [staged[pl.ds(0, half, stride=2), :], staged[pl.ds(1, half, stride=2), :]], axis=1
    ).astype(jnp.bfloat16)
    for i in range(out_ref.shape[0]):
        out_ref[i] = flat


def example_copies(n_copies, lengths, layer_inputs, out_grads, projections):
    both = projections.shape[2]
    rank = both // 2
    vmem = pl.BlockSpec(memory_space=pltpu.VMEM)
    return pl.pallas_call(
        example_kernel,
        out_shape=jax.ShapeDtypeStruct((n_copies, rank * rank // LANES, LANES), jnp.bfloat16),
        in_specs=[pl.BlockSpec(memory_space=pltpu.SMEM), vmem, vmem, vmem],
        out_specs=vmem,
        scratch_shapes=[pltpu.VMEM((rank, rank), jnp.float32)],
        compiler_params=pltpu.CompilerParams(vmem_limit_bytes=16 << 20),
        cost_estimate=pl.CostEstimate(
            flops=COST_FLOPS, bytes_accessed=9 << 20, transcendentals=0
        ),
        name="example_gradient",
    )(lengths, layer_inputs, out_grads, projections)


COST_FLOPS = 1 << 31


def score_kernel(n_sections, got_ref, *rest):
    block_refs, (out_ref, wide) = rest[:SIDE], rest[SIDE:]
    index = lax.axis_index("dp")
    x_pos, z_pos = lax.rem(index, SIDE), lax.div(index, SIDE * SIDE)
    n, rows, lanes = got_ref.shape
    wide[...] = got_ref[...].reshape(n * rows, lanes).astype(jnp.float32)
    examples = jnp.concatenate(
        [wide[pl.ds(c, n, stride=rows), :] for c in range(rows)], axis=1
    ).astype(jnp.bfloat16)
    queries = jnp.concatenate([b[...] for b in block_refs], axis=0)
    scores = lax.dot_general(
        examples, queries, (((1,), (1,)), ((), ())), preferred_element_type=jnp.float32
    )
    width = scores.shape[1] // SIDE
    scores = pltpu.roll(scores, lax.div(x_pos, 2) * (2 * width), 1)
    lane = lax.broadcasted_iota(jnp.int32, scores.shape, 1)
    paired = jnp.where(
        lax.rem(lax.div(lane, width), 2) == 0,
        pltpu.roll(scores, (SIDE - 1) * width, 1),
        pltpu.roll(scores, width, 1),
    )
    scores = jnp.where(lax.rem(x_pos, 2) == 1, paired, scores)
    for s in range(n_sections):
        row = (n_sections - 1 - s) * n
        out_ref[row : row + n, :] = jnp.where(z_pos == s, scores, jnp.zeros_like(scores))


def score_rows(n_sections, examples, blocks):
    n, rows, lanes = examples.shape
    vmem = pl.BlockSpec(memory_space=pltpu.VMEM)
    return pl.pallas_call(
        functools.partial(score_kernel, n_sections),
        out_shape=jax.ShapeDtypeStruct((n_sections * n, SIDE * blocks[0].shape[0]), jnp.float32),
        in_specs=[vmem] * (1 + SIDE),
        out_specs=vmem,
        scratch_shapes=[pltpu.VMEM((n * rows, lanes), jnp.float32)],
        compiler_params=pltpu.CompilerParams(vmem_limit_bytes=8 << 20),
        name="scores",
    )(examples, *blocks)


def total_kernel(got_ref, out_ref):
    n, lanes = got_ref.shape
    both = got_ref[0 : 2 * SIDE, :]
    for r in range(2 * SIDE, n, 2 * SIDE):
        both = both + got_ref[r : r + 2 * SIDE, :]
    for y in range(SIDE):
        r = SIDE - 1 - y
        out_ref[:, y * lanes : (y + 1) * lanes] = both[r : r + 1] + both[r + SIDE : r + SIDE + 1]


def total(got):
    vmem = pl.BlockSpec(memory_space=pltpu.VMEM)
    return pl.pallas_call(
        total_kernel,
        out_shape=jax.ShapeDtypeStruct((1, SIDE * got.shape[1]), jnp.float32),
        in_specs=[vmem],
        out_specs=vmem,
        compiler_params=pltpu.CompilerParams(vmem_limit_bytes=4 << 20),
        name="total",
    )(got)


def keep_kernel(in_ref, out_ref):
    out_ref[...] = in_ref[0]


def kept(block):
    vmem = pl.BlockSpec(memory_space=pltpu.VMEM)
    return pl.pallas_call(
        keep_kernel,
        out_shape=jax.ShapeDtypeStruct(block.shape[1:], block.dtype),
        in_specs=[vmem],
        out_specs=vmem,
        compiler_params=pltpu.CompilerParams(vmem_limit_bytes=4 << 20),
        cost_estimate=pl.CostEstimate(flops=COST_FLOPS * 8, bytes_accessed=9 << 20, transcendentals=0),
        name="own_queries",
    )(block)


def on_device(n_sections, n_dp, layer_inputs, out_grads, projections, query_grads, lengths):
    n_lines = n_dp // SIDE

    own = kept(query_grads)
    blocks = [own]
    for k in range(1, SIDE):
        pairs = []
        for s in range(n_sections):
            for line in range(n_lines):
                base = s * n_dp + line * SIDE
                pairs += [(base + x, base + (x ^ k)) for x in range(SIDE)]
        blocks.append(lax.ppermute(own, BOTH, pairs))

    lines = list(range(n_lines))[::-1]
    sections = list(range(n_sections))[::-1]

    plane = [[line * SIDE + x for line in lines] for x in range(SIDE)]
    copies = example_copies(n_lines, lengths, layer_inputs, out_grads, projections)
    examples = lax.all_to_all(copies, "dp", 0, 0, tiled=True, axis_index_groups=plane)

    send = score_rows(n_sections, examples, blocks)
    over = [[s * n_dp + line * SIDE + x for s in sections for line in lines] for x in range(SIDE)]
    got = lax.all_to_all(send[:, None], BOTH, 0, 0, tiled=True, axis_index_groups=over)
    return total(got.reshape(send.shape))


def solution(mesh):
    placed = (
        P("section", "dp", None, None),
        P("section", "dp", None, None),
        P("section", None, None),
        P("section", "dp", None),
        P("dp"),
    )

    def body(*args):
        return on_device(mesh.shape["section"], mesh.shape["dp"], *args)

    return jax.shard_map(
        body, mesh=mesh, in_specs=placed, out_specs=P("dp", "section"), check_vma=False
    )
```

time: 48.1 us -> 40.4 us (0.84)
  blocking collectives: 34.6 us -> 30.6 us
  Pallas kernels: 6.35 us -> 3.79 us
  starting transfers between devices: 5.64 us -> 4.07 us
  local copies, waits for them, and re-layouts: 0.01 us -> 1.11 us
  other arithmetic: 0.6 us -> 0 us
    all_to_all x1, blocking collectives: 16.1 us -> 12.7 us  [on_device(): lax.all_to_all(copies, 'dp', 0, 0, tiled=True, axis_index_groups=plane)]
    pallas_call x1, Pallas kernels: 5.9 us -> 2.66 us  [example_copies(): pl.pallas_call(example_kernel, out_shape=jax.ShapeDtypeStruct((n_copies,...]
    ppermute x3, starting transfers between devices: 5.64 us -> 4.07 us  [on_device(): blocks.append(lax.ppermute(own, BOTH, pairs))]
    unnamed x2 -> x8, local copies, waits for them, and re-layouts: 0.01 us -> 1.11 us
    pallas_call x0 -> x2, Pallas kernels: none -> 0.61 us  [the longest x1 0.59 us: total(): pl.pallas_call(total_kernel, out_shape=jax.ShapeDtypeStruct((1, SIDE * go...]
    reduce_sum x1 -> x0, other arithmetic: 0.6 us -> none  [on_device(): return got.sum((0, 1)).reshape(1, SIDE * send.shape[1])]
    all_to_all x1, blocking collectives: 18.4 us -> 17.9 us  [on_device(): lax.all_to_all(send[:, None], BOTH, 0, 0, tiled=True, axis_index_groups=o...]
  transfers between devices with their start and end apart: 3 -> 3, of which waited for: 0 -> 0; matrix products, arithmetic and copies ran while one was open for 0% -> 0% of each run, Pallas kernels for 12% -> 7%
where the time goes in v3:
time: 40.4 us; the launch traced here: 40.3 us
  blocking collectives  30.6 us (76%)
  starting transfers between devices  4.07 us (10%)
  Pallas kernels  3.79 us (9%)
  local copies, waits for them, and re-layouts  1.11 us (3%)
  between operations  0.7 us (2%)
    all_to_all x1, blocking collectives, on_device(): lax.all_to_all(send[:, None], BOTH, 0, 0, tiled=True, axis_index_groups=o...  17.9 us
    all_to_all x1, blocking collectives, on_device(): lax.all_to_all(copies, 'dp', 0, 0, tiled=True, axis_index_groups=plane)  12.7 us
    ppermute x3, starting transfers between devices, on_device(): blocks.append(lax.ppermute(own, BOTH, pairs))  4.07 us
    pallas_call x1, Pallas kernels, example_copies(): pl.pallas_call(example_kernel, out_shape=jax.ShapeDtypeStruct((n_copies,...  2.66 us
    unnamed x8, local copies, waits for them, and re-layouts  1.11 us
  transfers between devices with their start and end apart: 3, of which 0 were waited for; matrix products, arithmetic and copies ran while one was open for 0% of the time, Pallas kernels for 7%

profile of v3, /device:TPU:1, one launch (start us, length us, event | category | flops | bytes accessed | tf_op | source)
XLA Modules:
  0.0 40.3 jit_solution(10727504000151267464)
XLA Ops:
  0.0 0.0 copy-start.2
  0.0 0.0 copy-start.1
  0.0 0.0 copy-start.3
  0.0 1.1 %copy-done.3 = bf16[1,32,4096]{2,1,0:T(8,128)(2,1)S(1)} copy-done((bf16[1,32,4096]{2,1,0:T(8,128)(2,1)S(1)}, bf16[1,32,4096]{2,1,0:T(8,128)(2,1)}, u32[]{:S(2)}) %copy-start.3) | copy-done | bytes 262168
  1.1 0.0 copy-start
  1.1 3.4 %collective-permute-start.2 = (bf16[32,4096]{1,0:T(8,128)(2,1)S(1)}, bf16[32,4096]{1,0:T(8,128)(2,1)S(1)}, u32[]{:S(2)}, u32[]{:S(2)}) collective-permute-start(bf16[32,4096]{1,0:T(8,128)(2,1)S(1)} %own_queries.1.rest_0_), channel_id=1, source_target_pairs={{0,3},{1,2},{2,1},{3,0},{4,7},{5,6},{6,5},{7,4},{8,11},{9,10},{10,... | collective-permute-start | bytes 786440 | tf_op jit(solution)/shard_map/ppermute | solution.py:149
  4.5 0.5 %collective-permute-start.1 = (bf16[32,4096]{1,0:T(8,128)(2,1)S(1)}, bf16[32,4096]{1,0:T(8,128)(2,1)S(1)}, u32[]{:S(2)}, u32[]{:S(2)}) collective-permute-start(bf16[32,4096]{1,0:T(8,128)(2,1)S(1)} %own_queries.1.rest_0_), channel_id=1, source_target_pairs={{0,2},{1,3},{2,0},{3,1},{4,6},{5,7},{6,4},{7,5},{8,10},{9,11},{10,... | collective-permute-start | bytes 786440 | tf_op jit(solution)/shard_map/ppermute | solution.py:149
  5.0 0.2 collective-permute-start
  5.9 0.0 copy-done.2
  5.9 0.0 copy-done.1
  5.9 0.0 copy-done
  5.9 2.7 %example_gradient.1 = bf16[16,32,128]{2,1,0:T(8,128)(2,1)S(1)} custom-call(s32[1]{0:T(128)S(6)} %copy.7.len_ref, bf16[1,1,512,4096]{3,2,1,0:T(8,128)(2,1)S(1)} %copy-done, bf16[1,1,512,4096]{3,2,1,0:T(8,128)(2,1)S(1)} %copy-done.1, bf16[1,4096,128]{2,1,0:T(8,128)(2,1)S(1)} %copy-done.2), custom_call_target="tpu_custom_call" | custom-call | flops 2147483648 | bytes 9437184 | tf_op jit(solution)/shard_map/example_gradient/pallas_call | solution.py:41
  8.6 12.7 %all_to_all.10.got_ref = bf16[16,32,128]{2,1,0:T(8,128)(2,1)S(1)} all-to-all(bf16[16,32,128]{2,1,0:T(8,128)(2,1)S(1)} %example_gradient.1), channel_id=1, replica_groups={{60,56,52,48,44,40,36,32,28,24,20,16,12,8,4,0},{61,57,53,49,45,41,37,33..., dimensions={0} | all-to-all | bytes 262144 | tf_op jit(solution)/shard_map/all_to_all | solution.py:156
  21.3 0.0 collective-permute-done.2.rest_3_
  21.3 0.0 collective-permute-done.1.rest_2_
  21.3 0.0 collective-permute-done.rest_1_
  21.3 0.5 %scores.1 = f32[64,128]{1,0:T(8,128)S(1)} custom-call(bf16[16,32,128]{2,1,0:T(8,128)(2,1)S(1)} %all_to_all.10.got_ref, bf16[32,4096]{1,0:T(8,128)(2,1)S(1)} %own_queries.1.rest_0_, bf16[32,4096]{1,0:T(8,128)(2,1)S(1)} %collective-permute-done.rest_1_, bf16[32,4096]{1,0:T(8,128)(2,1)S(1)} %collective-permute-done.1.rest_2_, ...), custom_call_target="tpu_custom_call" | custom-call | tf_op jit(solution)/shard_map/scores/pallas_call | solution.py:88
  21.8 17.9 %all_to_all.11 = f32[64,1,128]{2,1,0:T(1,128)S(1)} all-to-all(f32[64,1,128]{2,1,0:T(1,128)S(1)} %bitcast.4), channel_id=1, replica_groups={{252,248,244,240,236,232,228,224,220,216,212,208,204,200,196,192,188,18..., dimensions={0} | all-to-all | bytes 65536 | tf_op jit(solution)/shard_map/all_to_all | solution.py:160
  39.7 0.6 %total.1 = f32[1,512]{1,0:T(1,128)} custom-call(f32[64,128]{1,0:T(8,128)S(1)} %bitcast.5), custom_call_target="tpu_custom_call" | custom-call | tf_op jit(solution)/shard_map/total/pallas_call | solution.py:111
  (1 shorter events, 0.0 us)
Async XLA Ops:
  0.0 5.9 %copy-start.2 = (bf16[1,4096,128]{2,1,0:T(8,128)(2,1)S(1)}, bf16[1,4096,128]{2,1,0:T(8,128)(2,1)}, u32[]{:S(2)}) copy-start(bf16[1,4096,128]{2,1,0:T(8,128)(2,1)} %proj_ref.1) | copy-start | bytes 3145732
  0.0 5.9 %copy-start.1 = (bf16[1,1,512,4096]{3,2,1,0:T(8,128)(2,1)S(1)}, bf16[1,1,512,4096]{3,2,1,0:T(8,128)(2,1)}, u32[]{:S(2)}) copy-start(bf16[1,1,512,4096]{3,2,1,0:T(8,128)(2,1)} %grad_ref.1) | copy-start | bytes 12582916
  0.0 1.1 %copy-start.3 = (bf16[1,32,4096]{2,1,0:T(8,128)(2,1)S(1)}, bf16[1,32,4096]{2,1,0:T(8,128)(2,1)}, u32[]{:S(2)}) copy-start(bf16[1,32,4096]{2,1,0:T(8,128)(2,1)} %in_ref.3) | copy-start | bytes 786436
  1.1 4.8 %copy-start = (bf16[1,1,512,4096]{3,2,1,0:T(8,128)(2,1)S(1)}, bf16[1,1,512,4096]{3,2,1,0:T(8,128)(2,1)}, u32[]{:S(2)}) copy-start(bf16[1,1,512,4096]{3,2,1,0:T(8,128)(2,1)} %in_ref.2) | copy-start | bytes 12582916
  1.1 20.1 %collective-permute-start.2 = (bf16[32,4096]{1,0:T(8,128)(2,1)S(1)}, bf16[32,4096]{1,0:T(8,128)(2,1)S(1)}, u32[]{:S(2)}, u32[]{:S(2)}) collective-permute-start(bf16[32,4096]{1,0:T(8,128)(2,1)S(1)} %own_queries.1.rest_0_), channel_id=1, source_target_pairs={{0,3},{1,2},{2,1},{3,0},{4,7},{5,6},{6,5},{7,4},{8,11},{9,10},{10,... | collective-permute-start | bytes 786440 | tf_op jit(solution)/shard_map/ppermute | solution.py:149
  4.5 16.7 %collective-permute-start.1 = (bf16[32,4096]{1,0:T(8,128)(2,1)S(1)}, bf16[32,4096]{1,0:T(8,128)(2,1)S(1)}, u32[]{:S(2)}, u32[]{:S(2)}) collective-permute-start(bf16[32,4096]{1,0:T(8,128)(2,1)S(1)} %own_queries.1.rest_0_), channel_id=1, source_target_pairs={{0,2},{1,3},{2,0},{3,1},{4,6},{5,7},{6,4},{7,5},{8,10},{9,11},{10,... | collective-permute-start | bytes 786440 | tf_op jit(solution)/shard_map/ppermute | solution.py:149
  5.0 16.2 %collective-permute-start = (bf16[32,4096]{1,0:T(8,128)(2,1)S(1)}, bf16[32,4096]{1,0:T(8,128)(2,1)S(1)}, u32[]{:S(2)}, u32[]{:S(2)}) collective-permute-start(bf16[32,4096]{1,0:T(8,128)(2,1)S(1)} %own_queries.1.rest_0_), channel_id=1, source_target_pairs={{0,1},{1,0},{2,3},{3,2},{4,5},{5,4},{6,7},{7,6},{8,9},{9,8},{10,11... | collective-permute-start | bytes 786440 | tf_op jit(solution)/shard_map/ppermute | solution.py:149

commit v4 on v3

--- a/solution.py
+++ b/solution.py
@@ -10,6 +10,7 @@
 SIDE = 4
 BOTH = ("section", "dp")
 LANES = 128
+ORDER = (2, 3, 1, 0)
 
 
 def example_kernel(len_ref, in_ref, grad_ref, proj_ref, out_ref, staged):
@@ -98,12 +99,14 @@
 
 def total_kernel(got_ref, out_ref):
     n, lanes = got_ref.shape
-    both = got_ref[0 : 2 * SIDE, :]
-    for r in range(2 * SIDE, n, 2 * SIDE):
-        both = both + got_ref[r : r + 2 * SIDE, :]
-    for y in range(SIDE):
-        r = SIDE - 1 - y
-        out_ref[:, y * lanes : (y + 1) * lanes] = both[r : r + 1] + both[r + SIDE : r + SIDE + 1]
+    lines = SIDE * SIDE
+    summed = got_ref[0:lines, :]
+    for r in range(lines, n, lines):
+        summed = summed + got_ref[r : r + lines, :]
+    for i, y in enumerate(ORDER):
+        out_ref[:, y * lanes : (y + 1) * lanes] = jnp.sum(
+            summed[i * SIDE : (i + 1) * SIDE], axis=0, keepdims=True
+        )
 
 
 def total(got):
@@ -148,7 +151,7 @@
                 pairs += [(base + x, base + (x ^ k)) for x in range(SIDE)]
         blocks.append(lax.ppermute(own, BOTH, pairs))
 
-    lines = list(range(n_lines))[::-1]
+    lines = [z * SIDE + y for y in ORDER for z in ORDER]
     sections = list(range(n_sections))[::-1]
 
     plane = [[line * SIDE + x for line in lines] for x in range(SIDE)]

time: 40.4 us -> 38.1 us (0.943)
  blocking collectives: 30.6 us -> 28.3 us
    all_to_all x1, blocking collectives: 17.9 us -> 15.4 us  [on_device(): lax.all_to_all(send[:, None], BOTH, 0, 0, tiled=True, axis_index_groups=o...]
where the time goes in v4:
time: 38.1 us; the launch traced here: 37.9 us
  blocking collectives  28.3 us (74%)
  starting transfers between devices  4.07 us (11%)
  Pallas kernels  3.79 us (10%)
  local copies, waits for them, and re-layouts  1.11 us (3%)
  between operations  0.7 us (2%)
    all_to_all x1, blocking collectives, on_device(): lax.all_to_all(send[:, None], BOTH, 0, 0, tiled=True, axis_index_groups=o...  15.4 us
    all_to_all x1, blocking collectives, on_device(): lax.all_to_all(copies, 'dp', 0, 0, tiled=True, axis_index_groups=plane)  12.8 us
    ppermute x3, starting transfers between devices, on_device(): blocks.append(lax.ppermute(own, BOTH, pairs))  4.07 us
    pallas_call x1, Pallas kernels, example_copies(): pl.pallas_call(example_kernel, out_shape=jax.ShapeDtypeStruct((n_copies,...  2.66 us
    unnamed x8, local copies, waits for them, and re-layouts  1.11 us
  transfers between devices with their start and end apart: 3, of which 0 were waited for; matrix products, arithmetic and copies ran while one was open for 0% of the time, Pallas kernels for 7%

profile of v4, /device:TPU:1, one launch (start us, length us, event | category | flops | bytes accessed | tf_op | source)
XLA Modules:
  0.0 37.9 jit_solution(12033865457144541851)
XLA Ops:
  0.0 0.0 copy-start.2
  0.0 0.0 copy-start.1
  0.0 0.0 copy-start.3
  0.0 1.1 %copy-done.3 = bf16[1,32,4096]{2,1,0:T(8,128)(2,1)S(1)} copy-done((bf16[1,32,4096]{2,1,0:T(8,128)(2,1)S(1)}, bf16[1,32,4096]{2,1,0:T(8,128)(2,1)}, u32[]{:S(2)}) %copy-start.3) | copy-done | bytes 262168
  1.1 0.0 copy-start
  1.1 3.4 %collective-permute-start.2 = (bf16[32,4096]{1,0:T(8,128)(2,1)S(1)}, bf16[32,4096]{1,0:T(8,128)(2,1)S(1)}, u32[]{:S(2)}, u32[]{:S(2)}) collective-permute-start(bf16[32,4096]{1,0:T(8,128)(2,1)S(1)} %own_queries.1.rest_0_), channel_id=1, source_target_pairs={{0,3},{1,2},{2,1},{3,0},{4,7},{5,6},{6,5},{7,4},{8,11},{9,10},{10,... | collective-permute-start | bytes 786440 | tf_op jit(solution)/shard_map/ppermute | solution.py:152
  4.5 0.5 %collective-permute-start.1 = (bf16[32,4096]{1,0:T(8,128)(2,1)S(1)}, bf16[32,4096]{1,0:T(8,128)(2,1)S(1)}, u32[]{:S(2)}, u32[]{:S(2)}) collective-permute-start(bf16[32,4096]{1,0:T(8,128)(2,1)S(1)} %own_queries.1.rest_0_), channel_id=1, source_target_pairs={{0,2},{1,3},{2,0},{3,1},{4,6},{5,7},{6,4},{7,5},{8,10},{9,11},{10,... | collective-permute-start | bytes 786440 | tf_op jit(solution)/shard_map/ppermute | solution.py:152
  5.0 0.2 collective-permute-start
  5.9 0.0 copy-done.2
  5.9 0.0 copy-done.1
  5.9 0.0 copy-done
  5.9 2.7 %example_gradient.1 = bf16[16,32,128]{2,1,0:T(8,128)(2,1)S(1)} custom-call(s32[1]{0:T(128)S(6)} %copy.7.len_ref, bf16[1,1,512,4096]{3,2,1,0:T(8,128)(2,1)S(1)} %copy-done, bf16[1,1,512,4096]{3,2,1,0:T(8,128)(2,1)S(1)} %copy-done.1, bf16[1,4096,128]{2,1,0:T(8,128)(2,1)S(1)} %copy-done.2), custom_call_target="tpu_custom_call" | custom-call | flops 2147483648 | bytes 9437184 | tf_op jit(solution)/shard_map/example_gradient/pallas_call | solution.py:42
  8.6 12.8 %all_to_all.10.got_ref = bf16[16,32,128]{2,1,0:T(8,128)(2,1)S(1)} all-to-all(bf16[16,32,128]{2,1,0:T(8,128)(2,1)S(1)} %example_gradient.1), channel_id=1, replica_groups={{40,56,24,8,44,60,28,12,36,52,20,4,32,48,16,0},{41,57,25,9,45,61,29,13,..., dimensions={0} | all-to-all | bytes 262144 | tf_op jit(solution)/shard_map/all_to_all | solution.py:159
  21.4 0.0 collective-permute-done.2.rest_3_
  21.4 0.0 collective-permute-done.1.rest_2_
  21.4 0.0 collective-permute-done.rest_1_
  21.4 0.5 %scores.1 = f32[64,128]{1,0:T(8,128)S(1)} custom-call(bf16[16,32,128]{2,1,0:T(8,128)(2,1)S(1)} %all_to_all.10.got_ref, bf16[32,4096]{1,0:T(8,128)(2,1)S(1)} %own_queries.1.rest_0_, bf16[32,4096]{1,0:T(8,128)(2,1)S(1)} %collective-permute-done.rest_1_, bf16[32,4096]{1,0:T(8,128)(2,1)S(1)} %collective-permute-done.1.rest_2_, ...), custom_call_target="tpu_custom_call" | custom-call | tf_op jit(solution)/shard_map/scores/pallas_call | solution.py:89
  21.9 15.4 %all_to_all.11 = f32[64,1,128]{2,1,0:T(1,128)S(1)} all-to-all(f32[64,1,128]{2,1,0:T(1,128)S(1)} %bitcast.4), channel_id=1, replica_groups={{232,248,216,200,236,252,220,204,228,244,212,196,224,240,208,192,168,18..., dimensions={0} | all-to-all | bytes 65536 | tf_op jit(solution)/shard_map/all_to_all | solution.py:163
  37.3 0.6 %total.1 = f32[1,512]{1,0:T(1,128)} custom-call(f32[64,128]{1,0:T(8,128)S(1)} %bitcast.5), custom_call_target="tpu_custom_call" | custom-call | tf_op jit(solution)/shard_map/total/pallas_call | solution.py:114
  (1 shorter events, 0.0 us)
Async XLA Ops:
  0.0 5.9 %copy-start.2 = (bf16[1,4096,128]{2,1,0:T(8,128)(2,1)S(1)}, bf16[1,4096,128]{2,1,0:T(8,128)(2,1)}, u32[]{:S(2)}) copy-start(bf16[1,4096,128]{2,1,0:T(8,128)(2,1)} %proj_ref.1) | copy-start | bytes 3145732
  0.0 5.9 %copy-start.1 = (bf16[1,1,512,4096]{3,2,1,0:T(8,128)(2,1)S(1)}, bf16[1,1,512,4096]{3,2,1,0:T(8,128)(2,1)}, u32[]{:S(2)}) copy-start(bf16[1,1,512,4096]{3,2,1,0:T(8,128)(2,1)} %grad_ref.1) | copy-start | bytes 12582916
  0.0 1.1 %copy-start.3 = (bf16[1,32,4096]{2,1,0:T(8,128)(2,1)S(1)}, bf16[1,32,4096]{2,1,0:T(8,128)(2,1)}, u32[]{:S(2)}) copy-start(bf16[1,32,4096]{2,1,0:T(8,128)(2,1)} %in_ref.3) | copy-start | bytes 786436
  1.1 4.8 %copy-start = (bf16[1,1,512,4096]{3,2,1,0:T(8,128)(2,1)S(1)}, bf16[1,1,512,4096]{3,2,1,0:T(8,128)(2,1)}, u32[]{:S(2)}) copy-start(bf16[1,1,512,4096]{3,2,1,0:T(8,128)(2,1)} %in_ref.2) | copy-start | bytes 12582916
  1.1 20.3 %collective-permute-start.2 = (bf16[32,4096]{1,0:T(8,128)(2,1)S(1)}, bf16[32,4096]{1,0:T(8,128)(2,1)S(1)}, u32[]{:S(2)}, u32[]{:S(2)}) collective-permute-start(bf16[32,4096]{1,0:T(8,128)(2,1)S(1)} %own_queries.1.rest_0_), channel_id=1, source_target_pairs={{0,3},{1,2},{2,1},{3,0},{4,7},{5,6},{6,5},{7,4},{8,11},{9,10},{10,... | collective-permute-start | bytes 786440 | tf_op jit(solution)/shard_map/ppermute | solution.py:152
  4.5 16.9 %collective-permute-start.1 = (bf16[32,4096]{1,0:T(8,128)(2,1)S(1)}, bf16[32,4096]{1,0:T(8,128)(2,1)S(1)}, u32[]{:S(2)}, u32[]{:S(2)}) collective-permute-start(bf16[32,4096]{1,0:T(8,128)(2,1)S(1)} %own_queries.1.rest_0_), channel_id=1, source_target_pairs={{0,2},{1,3},{2,0},{3,1},{4,6},{5,7},{6,4},{7,5},{8,10},{9,11},{10,... | collective-permute-start | bytes 786440 | tf_op jit(solution)/shard_map/ppermute | solution.py:152
  5.0 16.4 %collective-permute-start = (bf16[32,4096]{1,0:T(8,128)(2,1)S(1)}, bf16[32,4096]{1,0:T(8,128)(2,1)S(1)}, u32[]{:S(2)}, u32[]{:S(2)}) collective-permute-start(bf16[32,4096]{1,0:T(8,128)(2,1)S(1)} %own_queries.1.rest_0_), channel_id=1, source_target_pairs={{0,1},{1,0},{2,3},{3,2},{4,5},{5,4},{6,7},{7,6},{8,9},{9,8},{10,11... | collective-permute-start | bytes 786440 | tf_op jit(solution)/shard_map/ppermute | solution.py:152

commit v5 on v4

--- a/solution.py
+++ b/solution.py
@@ -97,7 +97,7 @@
     )(examples, *blocks)
 
 
-def total_kernel(got_ref, out_ref):
+def total_kernel(got_ref, marked_ref, out_ref):
     n, lanes = got_ref.shape
     lines = SIDE * SIDE
     summed = got_ref[0:lines, :]
@@ -109,39 +109,37 @@
         )
 
 
-def total(got):
+def total(got, marked):
     vmem = pl.BlockSpec(memory_space=pltpu.VMEM)
     return pl.pallas_call(
         total_kernel,
         out_shape=jax.ShapeDtypeStruct((1, SIDE * got.shape[1]), jnp.float32),
-        in_specs=[vmem],
+        in_specs=[vmem, pl.BlockSpec(memory_space=pl.ANY)],
         out_specs=vmem,
         compiler_params=pltpu.CompilerParams(vmem_limit_bytes=4 << 20),
         name="total",
-    )(got)
+    )(got, marked)
 
 
-def keep_kernel(in_ref, out_ref):
-    out_ref[...] = in_ref[0]
+def mark_kernel(out_ref):
+    del out_ref
 
 
-def kept(block):
-    vmem = pl.BlockSpec(memory_space=pltpu.VMEM)
+def mark():
     return pl.pallas_call(
-        keep_kernel,
-        out_shape=jax.ShapeDtypeStruct(block.shape[1:], block.dtype),
-        in_specs=[vmem],
-        out_specs=vmem,
-        compiler_params=pltpu.CompilerParams(vmem_limit_bytes=4 << 20),
-        cost_estimate=pl.CostEstimate(flops=COST_FLOPS * 8, bytes_accessed=9 << 20, transcendentals=0),
-        name="own_queries",
-    )(block)
+        mark_kernel,
+        out_shape=jax.ShapeDtypeStruct((8, LANES), jnp.int32),
+        out_specs=pl.BlockSpec(memory_space=pl.ANY),
+        compiler_params=pltpu.CompilerParams(vmem_limit_bytes=56064 << 10),
+        cost_estimate=pl.CostEstimate(flops=7 << 30, bytes_accessed=1 << 10, transcendentals=0),
+        name="mark",
+    )()
 
 
 def on_device(n_sections, n_dp, layer_inputs, out_grads, projections, query_grads, lengths):
     n_lines = n_dp // SIDE
 
-    own = kept(query_grads)
+    own, marked = lax.optimization_barrier((query_grads[0], mark()))
     blocks = [own]
     for k in range(1, SIDE):
         pairs = []
@@ -161,7 +159,7 @@
     send = score_rows(n_sections, examples, blocks)
     over = [[s * n_dp + line * SIDE + x for s in sections for line in lines] for x in range(SIDE)]
     got = lax.all_to_all(send[:, None], BOTH, 0, 0, tiled=True, axis_index_groups=over)
-    return total(got.reshape(send.shape))
+    return total(got.reshape(send.shape), marked)
 
 
 def solution(mesh):

time: 38.1 us -> 37 us (0.971)
  local copies, waits for them, and re-layouts: 1.11 us -> 0.02 us
    unnamed x8 -> x10, local copies, waits for them, and re-layouts: 1.11 us -> 0.02 us
where the time goes in v5:
time: 37 us; the launch traced here: 36.9 us
  blocking collectives  28.3 us (76%)
  starting transfers between devices  4.07 us (11%)
  Pallas kernels  3.78 us (10%)
  between operations  0.73 us (2%)
    all_to_all x1, blocking collectives, on_device(): lax.all_to_all(send[:, None], BOTH, 0, 0, tiled=True, axis_index_groups=o...  15.4 us
    all_to_all x1, blocking collectives, on_device(): lax.all_to_all(copies, 'dp', 0, 0, tiled=True, axis_index_groups=plane)  12.8 us
    ppermute x3, starting transfers between devices, on_device(): blocks.append(lax.ppermute(own, BOTH, pairs))  4.07 us
    pallas_call x1, Pallas kernels, example_copies(): pl.pallas_call(example_kernel, out_shape=jax.ShapeDtypeStruct((n_copies,...  2.66 us
  transfers between devices with their start and end apart: 3, of which 0 were waited for; matrix products, arithmetic and copies ran while one was open for 0% of the time, Pallas kernels for 7%

profile of v5, /device:TPU:1, one launch (start us, length us, event | category | flops | bytes accessed | tf_op | source)
XLA Modules:
  0.0 36.9 jit_solution(6047340743362000899)
XLA Ops:
  0.0 0.0 copy-start.2
  0.0 0.0 copy-start.1
  0.0 0.0 copy-start
  0.0 3.4 %collective-permute-start.2 = (bf16[32,4096]{1,0:T(8,128)(2,1)}, bf16[32,4096]{1,0:T(8,128)(2,1)S(1)}, u32[]{:S(2)}, u32[]{:S(2)}) collective-permute-start(bf16[32,4096]{1,0:T(8,128)(2,1)} %bitcast.5), channel_id=1, source_target_pairs={{0,3},{1,2},{2,1},{3,0},{4,7},{5,6},{6,5},{7,4},{8,11},{9,10},{10,... | collective-permute-start | bytes 786440 | tf_op jit(solution)/shard_map/ppermute | solution.py:150
  3.4 0.5 %collective-permute-start.1 = (bf16[32,4096]{1,0:T(8,128)(2,1)}, bf16[32,4096]{1,0:T(8,128)(2,1)S(1)}, u32[]{:S(2)}, u32[]{:S(2)}) collective-permute-start(bf16[32,4096]{1,0:T(8,128)(2,1)} %bitcast.6), channel_id=1, source_target_pairs={{0,2},{1,3},{2,0},{3,1},{4,6},{5,7},{6,4},{7,5},{8,10},{9,11},{10,... | collective-permute-start | bytes 786440 | tf_op jit(solution)/shard_map/ppermute | solution.py:150
  3.9 0.2 collective-permute-start
  4.7 0.0 copy-done.2
  4.8 0.0 copy-done.1
  4.8 0.0 copy-done
  4.8 0.0 copy-start.3
  4.8 0.0 copy-start.4
  4.8 2.7 %example_gradient.1 = bf16[16,32,128]{2,1,0:T(8,128)(2,1)S(1)} custom-call(s32[1]{0:T(128)S(6)} %copy.7.len_ref, bf16[1,1,512,4096]{3,2,1,0:T(8,128)(2,1)S(1)} %copy-done, bf16[1,1,512,4096]{3,2,1,0:T(8,128)(2,1)S(1)} %copy-done.1, bf16[1,4096,128]{2,1,0:T(8,128)(2,1)S(1)} %copy-done.2), custom_call_target="tpu_custom_call" | custom-call | flops 2147483648 | bytes 9437184 | tf_op jit(solution)/shard_map/example_gradient/pallas_call | solution.py:42
  7.5 12.8 %all_to_all.10.got_ref = bf16[16,32,128]{2,1,0:T(8,128)(2,1)S(1)} all-to-all(bf16[16,32,128]{2,1,0:T(8,128)(2,1)S(1)} %example_gradient.1), channel_id=1, replica_groups={{40,56,24,8,44,60,28,12,36,52,20,4,32,48,16,0},{41,57,25,9,45,61,29,13,..., dimensions={0} | all-to-all | bytes 262144 | tf_op jit(solution)/shard_map/all_to_all | solution.py:157
  20.3 0.0 collective-permute-done.2.rest_3_
  20.3 0.0 collective-permute-done.1.rest_2_
  20.3 0.0 collective-permute-done.rest_1_
  20.3 0.0 copy-done.3
  20.3 0.5 %scores.1 = f32[64,128]{1,0:T(8,128)S(1)} custom-call(bf16[16,32,128]{2,1,0:T(8,128)(2,1)S(1)} %all_to_all.10.got_ref, bf16[32,4096]{1,0:T(8,128)(2,1)S(1)} %bitcast.8, bf16[32,4096]{1,0:T(8,128)(2,1)S(1)} %collective-permute-done.rest_1_, bf16[32,4096]{1,0:T(8,128)(2,1)S(1)} %collective-permute-done.1.rest_2_, ...), custom_call_target="tpu_custom_call" | custom-call | tf_op jit(solution)/shard_map/scores/pallas_call | solution.py:89
  20.9 15.4 %all_to_all.11 = f32[64,1,128]{2,1,0:T(1,128)S(1)} all-to-all(f32[64,1,128]{2,1,0:T(1,128)S(1)} %bitcast.9), channel_id=1, replica_groups={{232,248,216,200,236,252,220,204,228,244,212,196,224,240,208,192,168,18..., dimensions={0} | all-to-all | bytes 65536 | tf_op jit(solution)/shard_map/all_to_all | solution.py:161
  36.3 0.0 copy-done.4
  36.3 0.6 %total.1 = f32[1,512]{1,0:T(1,128)} custom-call(f32[64,128]{1,0:T(8,128)S(1)} %bitcast.10, s32[8,128]{1,0:T(8,128)S(1)} %copy-done.4), custom_call_target="tpu_custom_call" | custom-call | tf_op jit(solution)/shard_map/total/pallas_call | solution.py:114
  (1 shorter events, 0.0 us)
Async XLA Ops:
  0.0 4.7 %copy-start.2 = (bf16[1,4096,128]{2,1,0:T(8,128)(2,1)S(1)}, bf16[1,4096,128]{2,1,0:T(8,128)(2,1)}, u32[]{:S(2)}) copy-start(bf16[1,4096,128]{2,1,0:T(8,128)(2,1)} %proj_ref.1) | copy-start | bytes 3145732
  0.0 4.8 %copy-start.1 = (bf16[1,1,512,4096]{3,2,1,0:T(8,128)(2,1)S(1)}, bf16[1,1,512,4096]{3,2,1,0:T(8,128)(2,1)}, u32[]{:S(2)}) copy-start(bf16[1,1,512,4096]{3,2,1,0:T(8,128)(2,1)} %grad_ref.1) | copy-start | bytes 12582916
  0.0 4.8 %copy-start = (bf16[1,1,512,4096]{3,2,1,0:T(8,128)(2,1)S(1)}, bf16[1,1,512,4096]{3,2,1,0:T(8,128)(2,1)}, u32[]{:S(2)}) copy-start(bf16[1,1,512,4096]{3,2,1,0:T(8,128)(2,1)} %in_ref.1) | copy-start | bytes 12582916
  0.0 20.3 %collective-permute-start.2 = (bf16[32,4096]{1,0:T(8,128)(2,1)}, bf16[32,4096]{1,0:T(8,128)(2,1)S(1)}, u32[]{:S(2)}, u32[]{:S(2)}) collective-permute-start(bf16[32,4096]{1,0:T(8,128)(2,1)} %bitcast.5), channel_id=1, source_target_pairs={{0,3},{1,2},{2,1},{3,0},{4,7},{5,6},{6,5},{7,4},{8,11},{9,10},{10,... | collective-permute-start | bytes 786440 | tf_op jit(solution)/shard_map/ppermute | solution.py:150
  3.4 16.9 %collective-permute-start.1 = (bf16[32,4096]{1,0:T(8,128)(2,1)}, bf16[32,4096]{1,0:T(8,128)(2,1)S(1)}, u32[]{:S(2)}, u32[]{:S(2)}) collective-permute-start(bf16[32,4096]{1,0:T(8,128)(2,1)} %bitcast.6), channel_id=1, source_target_pairs={{0,2},{1,3},{2,0},{3,1},{4,6},{5,7},{6,4},{7,5},{8,10},{9,11},{10,... | collective-permute-start | bytes 786440 | tf_op jit(solution)/shard_map/ppermute | solution.py:150
  3.9 16.4 %collective-permute-start = (bf16[32,4096]{1,0:T(8,128)(2,1)}, bf16[32,4096]{1,0:T(8,128)(2,1)S(1)}, u32[]{:S(2)}, u32[]{:S(2)}) collective-permute-start(bf16[32,4096]{1,0:T(8,128)(2,1)} %bitcast.7), channel_id=1, source_target_pairs={{0,1},{1,0},{2,3},{3,2},{4,5},{5,4},{6,7},{7,6},{8,9},{9,8},{10,11... | collective-permute-start | bytes 786440 | tf_op jit(solution)/shard_map/ppermute | solution.py:150
  4.8 15.5 %copy-start.3 = (bf16[1,32,4096]{2,1,0:T(8,128)(2,1)S(1)}, bf16[1,32,4096]{2,1,0:T(8,128)(2,1)}, u32[]{:S(2)}) copy-start(bf16[1,32,4096]{2,1,0:T(8,128)(2,1)} %param.8) | copy-start | bytes 786436
  4.8 31.5 %copy-start.4 = (s32[8,128]{1,0:T(8,128)S(1)}, s32[8,128]{1,0:T(8,128)}, u32[]{:S(2)}) copy-start(s32[8,128]{1,0:T(8,128)} %mark.1.marked_ref) | copy-start | bytes 12292

commit v6 on v5

--- a/solution.py
+++ b/solution.py
@@ -10,22 +10,32 @@
 SIDE = 4
 BOTH = ("section", "dp")
 LANES = 128
+CHUNKS = 4
 ORDER = (2, 3, 1, 0)
 
 
 def example_kernel(len_ref, in_ref, grad_ref, proj_ref, out_ref, staged):
-    rank = proj_ref.shape[2] // 2
-    table = proj_ref[0]
-    input_side = jnp.dot(in_ref[0, 0], table, preferred_element_type=jnp.float32)
-    grad_side = jnp.dot(grad_ref[0, 0], table, preferred_element_type=jnp.float32)
+    model, both = proj_ref.shape[1:]
+    rank, width = both // 2, model // CHUNKS
+    input_side = grad_side = None
+    for c in range(CHUNKS):
+        cols = slice(c * width, (c + 1) * width)
+        table = proj_ref[0, cols, :]
+        a = jnp.dot(in_ref[0, 0, :, cols], table, preferred_element_type=jnp.float32)
+        b = lax.dot_general(
+            jnp.transpose(table)[rank:],
+            grad_ref[0, 0, :, cols],
+            (((1,), (1,)), ((), ())),
+            preferred_element_type=jnp.float32,
+        )
+        input_side = a if input_side is None else input_side + a
+        grad_side = b if grad_side is None else grad_side + b
     input_side = input_side[:, :rank].astype(jnp.bfloat16)
-    grad_side = grad_side[:, rank:].astype(jnp.bfloat16)
+    grad_side = grad_side.astype(jnp.bfloat16)
     count = len_ref[0]
-    real = lax.broadcasted_iota(jnp.int32, grad_side.shape, 0) < count
+    real = lax.broadcasted_iota(jnp.int32, grad_side.shape, 1) < count
     grad_side = jnp.where(real, grad_side, jnp.zeros_like(grad_side))
-    summed = lax.dot_general(
-        grad_side, input_side, (((0,), (0,)), ((), ())), preferred_element_type=jnp.float32
-    )
+    summed = jnp.dot(grad_side, input_side, preferred_element_type=jnp.float32)
     staged[...] = summed / count.astype(jnp.float32)
     half = rank // 2
     flat = jnp.concatenate(

time: 37 us -> 36.9 us (level)
  no operation moved by 1% of the time
where the time goes in v6:
time: 36.9 us; the launch traced here: 36.8 us
  blocking collectives  28.3 us (77%)
  starting transfers between devices  4.07 us (11%)
  Pallas kernels  3.71 us (10%)
  between operations  0.73 us (2%)
    all_to_all x1, blocking collectives, on_device(): lax.all_to_all(send[:, None], BOTH, 0, 0, tiled=True, axis_index_groups=o...  15.4 us
    all_to_all x1, blocking collectives, on_device(): lax.all_to_all(copies, 'dp', 0, 0, tiled=True, axis_index_groups=plane)  12.8 us
    ppermute x3, starting transfers between devices, on_device(): blocks.append(lax.ppermute(own, BOTH, pairs))  4.07 us
    pallas_call x1, Pallas kernels, example_copies(): pl.pallas_call(example_kernel, out_shape=jax.ShapeDtypeStruct((n_copies,...  2.59 us
  transfers between devices with their start and end apart: 3, of which 0 were waited for; matrix products, arithmetic and copies ran while one was open for 0% of the time, Pallas kernels for 7%

profile of v6, /device:TPU:1, one launch (start us, length us, event | category | flops | bytes accessed | tf_op | source)
XLA Modules:
  0.0 36.8 jit_solution(17032914346962784204)
XLA Ops:
  0.0 0.0 copy-start.2
  0.0 0.0 copy-start.1
  0.0 0.0 copy-start
  0.0 3.4 %collective-permute-start.2 = (bf16[32,4096]{1,0:T(8,128)(2,1)}, bf16[32,4096]{1,0:T(8,128)(2,1)S(1)}, u32[]{:S(2)}, u32[]{:S(2)}) collective-permute-start(bf16[32,4096]{1,0:T(8,128)(2,1)} %bitcast.5), channel_id=1, source_target_pairs={{0,3},{1,2},{2,1},{3,0},{4,7},{5,6},{6,5},{7,4},{8,11},{9,10},{10,... | collective-permute-start | bytes 786440 | tf_op jit(solution)/shard_map/ppermute | solution.py:160
  3.4 0.5 %collective-permute-start.1 = (bf16[32,4096]{1,0:T(8,128)(2,1)}, bf16[32,4096]{1,0:T(8,128)(2,1)S(1)}, u32[]{:S(2)}, u32[]{:S(2)}) collective-permute-start(bf16[32,4096]{1,0:T(8,128)(2,1)} %bitcast.6), channel_id=1, source_target_pairs={{0,2},{1,3},{2,0},{3,1},{4,6},{5,7},{6,4},{7,5},{8,10},{9,11},{10,... | collective-permute-start | bytes 786440 | tf_op jit(solution)/shard_map/ppermute | solution.py:160
  3.9 0.2 collective-permute-start
  4.7 0.0 copy-done.2
  4.8 0.0 copy-done.1
  4.8 0.0 copy-done
  4.8 0.0 copy-start.3
  4.8 0.0 copy-start.4
  4.8 2.6 %example_gradient.1 = bf16[16,32,128]{2,1,0:T(8,128)(2,1)S(1)} custom-call(s32[1]{0:T(128)S(6)} %copy.7.len_ref, bf16[1,1,512,4096]{3,2,1,0:T(8,128)(2,1)S(1)} %copy-done, bf16[1,1,512,4096]{3,2,1,0:T(8,128)(2,1)S(1)} %copy-done.1, bf16[1,4096,128]{2,1,0:T(8,128)(2,1)S(1)} %copy-done.2), custom_call_target="tpu_custom_call" | custom-call | flops 2147483648 | bytes 9437184 | tf_op jit(solution)/shard_map/example_gradient/pallas_call | solution.py:52
  7.4 12.8 %all_to_all.10.got_ref = bf16[16,32,128]{2,1,0:T(8,128)(2,1)S(1)} all-to-all(bf16[16,32,128]{2,1,0:T(8,128)(2,1)S(1)} %example_gradient.1), channel_id=1, replica_groups={{40,56,24,8,44,60,28,12,36,52,20,4,32,48,16,0},{41,57,25,9,45,61,29,13,..., dimensions={0} | all-to-all | bytes 262144 | tf_op jit(solution)/shard_map/all_to_all | solution.py:167
  20.2 0.0 collective-permute-done.2.rest_3_
  20.2 0.0 collective-permute-done.1.rest_2_
  20.2 0.0 collective-permute-done.rest_1_
  20.2 0.0 copy-done.3
  20.3 0.5 %scores.1 = f32[64,128]{1,0:T(8,128)S(1)} custom-call(bf16[16,32,128]{2,1,0:T(8,128)(2,1)S(1)} %all_to_all.10.got_ref, bf16[32,4096]{1,0:T(8,128)(2,1)S(1)} %bitcast.8, bf16[32,4096]{1,0:T(8,128)(2,1)S(1)} %collective-permute-done.rest_1_, bf16[32,4096]{1,0:T(8,128)(2,1)S(1)} %collective-permute-done.1.rest_2_, ...), custom_call_target="tpu_custom_call" | custom-call | tf_op jit(solution)/shard_map/scores/pallas_call | solution.py:99
  20.8 15.4 %all_to_all.11 = f32[64,1,128]{2,1,0:T(1,128)S(1)} all-to-all(f32[64,1,128]{2,1,0:T(1,128)S(1)} %bitcast.9), channel_id=1, replica_groups={{232,248,216,200,236,252,220,204,228,244,212,196,224,240,208,192,168,18..., dimensions={0} | all-to-all | bytes 65536 | tf_op jit(solution)/shard_map/all_to_all | solution.py:171
  36.2 0.0 copy-done.4
  36.2 0.6 %total.1 = f32[1,512]{1,0:T(1,128)} custom-call(f32[64,128]{1,0:T(8,128)S(1)} %bitcast.10, s32[8,128]{1,0:T(8,128)S(1)} %copy-done.4), custom_call_target="tpu_custom_call" | custom-call | tf_op jit(solution)/shard_map/total/pallas_call | solution.py:124
  (1 shorter events, 0.0 us)
Async XLA Ops:
  0.0 4.7 %copy-start.2 = (bf16[1,4096,128]{2,1,0:T(8,128)(2,1)S(1)}, bf16[1,4096,128]{2,1,0:T(8,128)(2,1)}, u32[]{:S(2)}) copy-start(bf16[1,4096,128]{2,1,0:T(8,128)(2,1)} %proj_ref.1) | copy-start | bytes 3145732
  0.0 4.8 %copy-start.1 = (bf16[1,1,512,4096]{3,2,1,0:T(8,128)(2,1)S(1)}, bf16[1,1,512,4096]{3,2,1,0:T(8,128)(2,1)}, u32[]{:S(2)}) copy-start(bf16[1,1,512,4096]{3,2,1,0:T(8,128)(2,1)} %grad_ref.1) | copy-start | bytes 12582916
  0.0 4.8 %copy-start = (bf16[1,1,512,4096]{3,2,1,0:T(8,128)(2,1)S(1)}, bf16[1,1,512,4096]{3,2,1,0:T(8,128)(2,1)}, u32[]{:S(2)}) copy-start(bf16[1,1,512,4096]{3,2,1,0:T(8,128)(2,1)} %in_ref.1) | copy-start | bytes 12582916
  0.0 20.2 %collective-permute-start.2 = (bf16[32,4096]{1,0:T(8,128)(2,1)}, bf16[32,4096]{1,0:T(8,128)(2,1)S(1)}, u32[]{:S(2)}, u32[]{:S(2)}) collective-permute-start(bf16[32,4096]{1,0:T(8,128)(2,1)} %bitcast.5), channel_id=1, source_target_pairs={{0,3},{1,2},{2,1},{3,0},{4,7},{5,6},{6,5},{7,4},{8,11},{9,10},{10,... | collective-permute-start | bytes 786440 | tf_op jit(solution)/shard_map/ppermute | solution.py:160
  3.4 16.8 %collective-permute-start.1 = (bf16[32,4096]{1,0:T(8,128)(2,1)}, bf16[32,4096]{1,0:T(8,128)(2,1)S(1)}, u32[]{:S(2)}, u32[]{:S(2)}) collective-permute-start(bf16[32,4096]{1,0:T(8,128)(2,1)} %bitcast.6), channel_id=1, source_target_pairs={{0,2},{1,3},{2,0},{3,1},{4,6},{5,7},{6,4},{7,5},{8,10},{9,11},{10,... | collective-permute-start | bytes 786440 | tf_op jit(solution)/shard_map/ppermute | solution.py:160
  3.9 16.3 %collective-permute-start = (bf16[32,4096]{1,0:T(8,128)(2,1)}, bf16[32,4096]{1,0:T(8,128)(2,1)S(1)}, u32[]{:S(2)}, u32[]{:S(2)}) collective-permute-start(bf16[32,4096]{1,0:T(8,128)(2,1)} %bitcast.7), channel_id=1, source_target_pairs={{0,1},{1,0},{2,3},{3,2},{4,5},{5,4},{6,7},{7,6},{8,9},{9,8},{10,11... | collective-permute-start | bytes 786440 | tf_op jit(solution)/shard_map/ppermute | solution.py:160
  4.8 15.5 %copy-start.3 = (bf16[1,32,4096]{2,1,0:T(8,128)(2,1)S(1)}, bf16[1,32,4096]{2,1,0:T(8,128)(2,1)}, u32[]{:S(2)}) copy-start(bf16[1,32,4096]{2,1,0:T(8,128)(2,1)} %param.8) | copy-start | bytes 786436
  4.8 31.4 %copy-start.4 = (s32[8,128]{1,0:T(8,128)S(1)}, s32[8,128]{1,0:T(8,128)}, u32[]{:S(2)}) copy-start(s32[8,128]{1,0:T(8,128)} %mark.1.marked_ref) | copy-start | bytes 12292

commit v7 on v6

--- a/solution.py
+++ b/solution.py
@@ -12,6 +12,10 @@
 LANES = 128
 CHUNKS = 4
 ORDER = (2, 3, 1, 0)
+
+
+def section_order(n_sections):
+    return sorted(range(n_sections), key=lambda s: (-(s % 2), -s))
 
 
 def example_kernel(len_ref, in_ref, grad_ref, proj_ref, out_ref, staged):
@@ -89,7 +93,7 @@
     )
     scores = jnp.where(lax.rem(x_pos, 2) == 1, paired, scores)
     for s in range(n_sections):
-        row = (n_sections - 1 - s) * n
+        row = section_order(n_sections).index(s) * n
         out_ref[row : row + n, :] = jnp.where(z_pos == s, scores, jnp.zeros_like(scores))
 
 
@@ -160,7 +164,7 @@
         blocks.append(lax.ppermute(own, BOTH, pairs))
 
     lines = [z * SIDE + y for y in ORDER for z in ORDER]
-    sections = list(range(n_sections))[::-1]
+    sections = section_order(n_sections)
 
     plane = [[line * SIDE + x for line in lines] for x in range(SIDE)]
     copies = example_copies(n_lines, lengths, layer_inputs, out_grads, projections)

time: 36.9 us -> 37 us (level)
  no operation moved by 1% of the time
where the time goes in v7:
time: 37 us; the launch traced here: 36.8 us
  blocking collectives  28.3 us (76%)
  starting transfers between devices  4.07 us (11%)
  Pallas kernels  3.71 us (10%)
  between operations  0.73 us (2%)
    all_to_all x1, blocking collectives, on_device(): lax.all_to_all(send[:, None], BOTH, 0, 0, tiled=True, axis_index_groups=o...  15.5 us
    all_to_all x1, blocking collectives, on_device(): lax.all_to_all(copies, 'dp', 0, 0, tiled=True, axis_index_groups=plane)  12.8 us
    ppermute x3, starting transfers between devices, on_device(): blocks.append(lax.ppermute(own, BOTH, pairs))  4.07 us
    pallas_call x1, Pallas kernels, example_copies(): pl.pallas_call(example_kernel, out_shape=jax.ShapeDtypeStruct((n_copies,...  2.59 us
  transfers between devices with their start and end apart: 3, of which 0 were waited for; matrix products, arithmetic and copies ran while one was open for 0% of the time, Pallas kernels for 7%

profile of v7, /device:TPU:1, one launch (start us, length us, event | category | flops | bytes accessed | tf_op | source)
XLA Modules:
  0.0 36.8 jit_solution(12905521038688582071)
XLA Ops:
  0.0 0.0 copy-start.2
  0.0 0.0 copy-start.1
  0.0 0.0 copy-start
  0.0 3.4 %collective-permute-start.2 = (bf16[32,4096]{1,0:T(8,128)(2,1)}, bf16[32,4096]{1,0:T(8,128)(2,1)S(1)}, u32[]{:S(2)}, u32[]{:S(2)}) collective-permute-start(bf16[32,4096]{1,0:T(8,128)(2,1)} %bitcast.5), channel_id=1, source_target_pairs={{0,3},{1,2},{2,1},{3,0},{4,7},{5,6},{6,5},{7,4},{8,11},{9,10},{10,... | collective-permute-start | bytes 786440 | tf_op jit(solution)/shard_map/ppermute | solution.py:164
  3.4 0.5 %collective-permute-start.1 = (bf16[32,4096]{1,0:T(8,128)(2,1)}, bf16[32,4096]{1,0:T(8,128)(2,1)S(1)}, u32[]{:S(2)}, u32[]{:S(2)}) collective-permute-start(bf16[32,4096]{1,0:T(8,128)(2,1)} %bitcast.6), channel_id=1, source_target_pairs={{0,2},{1,3},{2,0},{3,1},{4,6},{5,7},{6,4},{7,5},{8,10},{9,11},{10,... | collective-permute-start | bytes 786440 | tf_op jit(solution)/shard_map/ppermute | solution.py:164
  3.9 0.2 collective-permute-start
  4.7 0.0 copy-done.2
  4.8 0.0 copy-done.1
  4.8 0.0 copy-done
  4.8 0.0 copy-start.3
  4.8 0.0 copy-start.4
  4.8 2.6 %example_gradient.1 = bf16[16,32,128]{2,1,0:T(8,128)(2,1)S(1)} custom-call(s32[1]{0:T(128)S(6)} %copy.7.len_ref, bf16[1,1,512,4096]{3,2,1,0:T(8,128)(2,1)S(1)} %copy-done, bf16[1,1,512,4096]{3,2,1,0:T(8,128)(2,1)S(1)} %copy-done.1, bf16[1,4096,128]{2,1,0:T(8,128)(2,1)S(1)} %copy-done.2), custom_call_target="tpu_custom_call" | custom-call | flops 2147483648 | bytes 9437184 | tf_op jit(solution)/shard_map/example_gradient/pallas_call | solution.py:56
  7.4 12.8 %all_to_all.10.got_ref = bf16[16,32,128]{2,1,0:T(8,128)(2,1)S(1)} all-to-all(bf16[16,32,128]{2,1,0:T(8,128)(2,1)S(1)} %example_gradient.1), channel_id=1, replica_groups={{40,56,24,8,44,60,28,12,36,52,20,4,32,48,16,0},{41,57,25,9,45,61,29,13,..., dimensions={0} | all-to-all | bytes 262144 | tf_op jit(solution)/shard_map/all_to_all | solution.py:171
  20.2 0.0 collective-permute-done.2.rest_3_
  20.2 0.0 collective-permute-done.1.rest_2_
  20.2 0.0 collective-permute-done.rest_1_
  20.2 0.0 copy-done.3
  20.3 0.5 %scores.1 = f32[64,128]{1,0:T(8,128)S(1)} custom-call(bf16[16,32,128]{2,1,0:T(8,128)(2,1)S(1)} %all_to_all.10.got_ref, bf16[32,4096]{1,0:T(8,128)(2,1)S(1)} %bitcast.8, bf16[32,4096]{1,0:T(8,128)(2,1)S(1)} %collective-permute-done.rest_1_, bf16[32,4096]{1,0:T(8,128)(2,1)S(1)} %collective-permute-done.1.rest_2_, ...), custom_call_target="tpu_custom_call" | custom-call | tf_op jit(solution)/shard_map/scores/pallas_call | solution.py:103
  20.8 15.5 %all_to_all.11 = f32[64,1,128]{2,1,0:T(1,128)S(1)} all-to-all(f32[64,1,128]{2,1,0:T(1,128)S(1)} %bitcast.9), channel_id=1, replica_groups={{232,248,216,200,236,252,220,204,228,244,212,196,224,240,208,192,104,12..., dimensions={0} | all-to-all | bytes 65536 | tf_op jit(solution)/shard_map/all_to_all | solution.py:175
  36.3 0.0 copy-done.4
  36.3 0.6 %total.1 = f32[1,512]{1,0:T(1,128)} custom-call(f32[64,128]{1,0:T(8,128)S(1)} %bitcast.10, s32[8,128]{1,0:T(8,128)S(1)} %copy-done.4), custom_call_target="tpu_custom_call" | custom-call | tf_op jit(solution)/shard_map/total/pallas_call | solution.py:128
  (1 shorter events, 0.0 us)
Async XLA Ops:
  0.0 4.7 %copy-start.2 = (bf16[1,4096,128]{2,1,0:T(8,128)(2,1)S(1)}, bf16[1,4096,128]{2,1,0:T(8,128)(2,1)}, u32[]{:S(2)}) copy-start(bf16[1,4096,128]{2,1,0:T(8,128)(2,1)} %proj_ref.1) | copy-start | bytes 3145732
  0.0 4.8 %copy-start.1 = (bf16[1,1,512,4096]{3,2,1,0:T(8,128)(2,1)S(1)}, bf16[1,1,512,4096]{3,2,1,0:T(8,128)(2,1)}, u32[]{:S(2)}) copy-start(bf16[1,1,512,4096]{3,2,1,0:T(8,128)(2,1)} %grad_ref.1) | copy-start | bytes 12582916
  0.0 4.8 %copy-start = (bf16[1,1,512,4096]{3,2,1,0:T(8,128)(2,1)S(1)}, bf16[1,1,512,4096]{3,2,1,0:T(8,128)(2,1)}, u32[]{:S(2)}) copy-start(bf16[1,1,512,4096]{3,2,1,0:T(8,128)(2,1)} %in_ref.1) | copy-start | bytes 12582916
  0.0 20.2 %collective-permute-start.2 = (bf16[32,4096]{1,0:T(8,128)(2,1)}, bf16[32,4096]{1,0:T(8,128)(2,1)S(1)}, u32[]{:S(2)}, u32[]{:S(2)}) collective-permute-start(bf16[32,4096]{1,0:T(8,128)(2,1)} %bitcast.5), channel_id=1, source_target_pairs={{0,3},{1,2},{2,1},{3,0},{4,7},{5,6},{6,5},{7,4},{8,11},{9,10},{10,... | collective-permute-start | bytes 786440 | tf_op jit(solution)/shard_map/ppermute | solution.py:164
  3.4 16.8 %collective-permute-start.1 = (bf16[32,4096]{1,0:T(8,128)(2,1)}, bf16[32,4096]{1,0:T(8,128)(2,1)S(1)}, u32[]{:S(2)}, u32[]{:S(2)}) collective-permute-start(bf16[32,4096]{1,0:T(8,128)(2,1)} %bitcast.6), channel_id=1, source_target_pairs={{0,2},{1,3},{2,0},{3,1},{4,6},{5,7},{6,4},{7,5},{8,10},{9,11},{10,... | collective-permute-start | bytes 786440 | tf_op jit(solution)/shard_map/ppermute | solution.py:164
  3.9 16.3 %collective-permute-start = (bf16[32,4096]{1,0:T(8,128)(2,1)}, bf16[32,4096]{1,0:T(8,128)(2,1)S(1)}, u32[]{:S(2)}, u32[]{:S(2)}) collective-permute-start(bf16[32,4096]{1,0:T(8,128)(2,1)} %bitcast.7), channel_id=1, source_target_pairs={{0,1},{1,0},{2,3},{3,2},{4,5},{5,4},{6,7},{7,6},{8,9},{9,8},{10,11... | collective-permute-start | bytes 786440 | tf_op jit(solution)/shard_map/ppermute | solution.py:164
  4.8 15.5 %copy-start.3 = (bf16[1,32,4096]{2,1,0:T(8,128)(2,1)S(1)}, bf16[1,32,4096]{2,1,0:T(8,128)(2,1)}, u32[]{:S(2)}) copy-start(bf16[1,32,4096]{2,1,0:T(8,128)(2,1)} %param.8) | copy-start | bytes 786436
  4.8 31.5 %copy-start.4 = (s32[8,128]{1,0:T(8,128)S(1)}, s32[8,128]{1,0:T(8,128)}, u32[]{:S(2)}) copy-start(s32[8,128]{1,0:T(8,128)} %mark.1.marked_ref) | copy-start | bytes 12292
